TPU v7x, 128 devices: a whole 4x4x4 slice. The times are simulated.
128 devices in a mesh: row: 16 (over x_hi, y, core), col: 8 (over z, x_lo).
Axes of the slice: x: 4 (x_hi: 2, x_lo: 2; x = x_hi * 2 + x_lo), y: 4, z: 4, core: 2. Of those that a mesh axis runs over, the one named last changes fastest.
Arguments:
- values: float32 [8192, 8192], P('row', 'col'), may hold values from 0 to 10, as said below
- pattern: int32 [64, 64], replicated, may hold values from 0 to 1, as said below
- pruning: int32 [64, 64], replicated, may hold values from 0 to 1, as said below
- owners: int32 [64], replicated, may hold values from 0 to 63, as said below
Outputs:
- expanded: float32 [8192, 8192], P('row', 'col')
Inputs may be any that keep to these rules, and one draw needn't show every extreme that they name: `values`: positive scores. `pattern`: every diagonal block is present. `pruning`: every diagonal block is kept. `owners`: A permutation of the 64 column blocks. Of the 8 column blocks of one index of col, at most 2 are stored at the column blocks of any one index of col, and exactly 2 at those of some index.
All inputs are finite; a program needn't handle non-finite values.
Results may differ from a plain program's by a relative error of at most 0.00065.
Values may be sent and summed in bfloat16 or wider, within the bound.
No kernel may reach another device: no remote copies, remote signals or barrier semaphores. Data moves between devices by JAX's collectives and lax.ppermute only.
A program may use at most 128 MiB of HBM per device.

v0:
```python
import jax
import jax.numpy as jnp
from jax import lax
from jax.experimental import pallas as pl
from jax.experimental.pallas import tpu as pltpu
from jax.sharding import PartitionSpec as P


BLK = 128
ROWS = 512
COLS = 1024
NC = 8
NR = 16
CAP = 2
AXES = ("row", "col")


def decode(i):
    r, c = divmod(i, NC)
    return {"xh": r >> 3, "y": (r >> 1) & 3, "t": r & 1, "z": c >> 1, "xl": c & 1}


def encode(d):
    return ((d["xh"] << 3) | (d["y"] << 1) | d["t"]) * NC + ((d["z"] << 1) | d["xl"])


def flip(axis):
    out = []
    for i in range(NR * NC):
        d = decode(i)
        d[axis] ^= 1
        out.append((i, encode(d)))
    return out


def spread(axis):
    out = []
    for i in range(NR * NC):
        d = decode(i)
        d[axis] = (d[axis] + (1 if d["t"] == 0 else -1)) % 4
        out.append((i, encode(d)))
    return out


def send(x, pairs):
    return lax.ppermute(x, AXES, pairs)


def mask_kernel(keep_ref, v_ref, m_ref, ma_ref, mb_ref, p_ref):
    i = pl.program_id(0)

    @pl.when(i == 0)
    def _():
        p_ref[...] = jnp.zeros_like(p_ref)

    for j in range(COLS // BLK):
        sl = pl.ds(j * BLK, BLK)
        v = v_ref[:, sl]
        v = jnp.where(keep_ref[i, j] != 0, v, jnp.zeros_like(v))
        m = v.astype(jnp.bfloat16)
        m_ref[:, sl] = m

        @pl.when(i < 2)
        def _():
            ma_ref[:, sl] = m

        @pl.when(i >= 2)
        def _():
            mb_ref[:, sl] = m

        p_ref[:, sl] += jnp.sum(v.reshape(BLK // 8, 8, BLK), axis=0)


def mask_and_sum(values, keep):
    return pl.pallas_call(
        mask_kernel,
        grid_spec=pltpu.PrefetchScalarGridSpec(
            num_scalar_prefetch=1,
            grid=(ROWS // BLK,),
            in_specs=[pl.BlockSpec((BLK, COLS), lambda i, k: (i, 0))],
            out_specs=[
                pl.BlockSpec((BLK, COLS), lambda i, k: (i, 0)),
                pl.BlockSpec((BLK, COLS), lambda i, k: (jnp.minimum(i, 1), 0)),
                pl.BlockSpec((BLK, COLS), lambda i, k: (jnp.maximum(i, 2) - 2, 0)),
                pl.BlockSpec((8, COLS), lambda i, k: (0, 0)),
            ],
        ),
        out_shape=[
            jax.ShapeDtypeStruct((ROWS, COLS), jnp.bfloat16),
            jax.ShapeDtypeStruct((ROWS // 2, COLS), jnp.bfloat16),
            jax.ShapeDtypeStruct((ROWS // 2, COLS), jnp.bfloat16),
            jax.ShapeDtypeStruct((8, COLS), jnp.float32),
        ],
    )(keep, values)


def square_kernel(meta, keep, inv_ref, *refs):
    a_refs, b_refs = refs[:8], refs[8:24]
    h_ref, p_ref = refs[24:26]
    a_buf, b_buf, acc, a_sem, b_sem = refs[26:]
    xh, y, t, z, xl = (meta[i] for i in range(5))
    step = 2 * t - 1
    copies_a = []
    for i in range(8):
        dz = (0, step, -step, 2)[i % 4]
        c = ((z + dz) & 3) * 2 + (xl ^ (i // 4))
        copies_a.append(pltpu.make_async_copy(a_refs[i], a_buf.at[c], a_sem.at[i]))
    lo, hi = pl.multiple_of(t * ROWS, ROWS), pl.multiple_of((1 - t) * ROWS, ROWS)
    order = []
    for i in range(8):
        dy = (0, step, -step, 2)[i % 4]
        c = (xh ^ (i // 4)) * 4 + ((y + dy) & 3)
        group = []
        for k, at in ((2 * i, lo), (2 * i + 1, hi)):
            dst = b_buf.at[c, pl.ds(at, ROWS)]
            group.append(pltpu.make_async_copy(b_refs[k], dst, b_sem.at[k]))
        order.append((c, group))
    for copy in copies_a:
        copy.start()
    for _, group in order:
        for copy in group:
            copy.start()
    for copy in copies_a:
        copy.wait()
    for n, (c, group) in enumerate(order):
        for copy in group:
            copy.wait()
        a = (a_buf[c].astype(jnp.float32) * inv_ref[pl.ds(c, 1), :]).astype(jnp.bfloat16)
        part = jnp.dot(a, b_buf[c], preferred_element_type=jnp.float32)
        if n == 0:
            acc[...] = part
        else:
            acc[...] += part
    scale = inv_ref[pl.ds(z * 2 + xl, 1), :]
    for j in range(NC):
        sl = pl.ds(j * BLK, BLK)
        total = jnp.zeros((8, BLK), jnp.float32)
        for i in range(ROWS // BLK):
            rows = pl.ds(i * BLK, BLK)
            g = acc[rows, sl] * scale[:, j * BLK : (j + 1) * BLK]
            g = jnp.where(keep[i * NC + j] != 0, g * g, jnp.zeros_like(g))
            h_ref[j, rows] = g
            total += jnp.sum(g.reshape(BLK // 8, 8, BLK), axis=0)
        p_ref[pl.ds(j, 1), :] = jnp.sum(total, axis=0, keepdims=True)


def square_of(meta, keep, inv, a_pieces, b_pieces):
    anywhere = pl.BlockSpec(memory_space=pl.ANY)
    smem = pl.BlockSpec(memory_space=pltpu.SMEM)
    return pl.pallas_call(
        square_kernel,
        in_specs=[smem, smem, pl.BlockSpec(memory_space=pltpu.VMEM)] + [anywhere] * 24,
        out_specs=[pl.BlockSpec(memory_space=pltpu.VMEM)] * 2,
        out_shape=[
            jax.ShapeDtypeStruct((NC, ROWS, BLK), jnp.float32),
            jax.ShapeDtypeStruct((NC, BLK), jnp.float32),
        ],
        scratch_shapes=[
            pltpu.VMEM((NC, ROWS, COLS), jnp.bfloat16),
            pltpu.VMEM((NC, 2 * ROWS, COLS), jnp.bfloat16),
            pltpu.VMEM((ROWS, COLS), jnp.float32),
            pltpu.SemaphoreType.DMA((8,)),
            pltpu.SemaphoreType.DMA((16,)),
        ],
    )(meta, keep, inv, *a_pieces, *b_pieces)


def slot_tables(owners, me_col):
    table = owners.reshape(NC, NC)
    dest = table // NC
    earlier = jnp.arange(NC)[:, None] < jnp.arange(NC)[None, :]
    same = dest[:, :, None] == dest[:, None, :]
    rank = jnp.sum(jnp.where(same & earlier, 1, 0), axis=1)
    slots = jnp.arange(NC * CAP)
    mine = lax.dynamic_slice(dest, (me_col, 0), (1, NC))[0]
    my_rank = lax.dynamic_slice(rank, (me_col, 0), (1, NC))[0]
    hit = (mine[None, :] * CAP + my_rank[None, :]) == slots[:, None]
    outgoing = jnp.sum(jnp.where(hit, jnp.arange(NC)[None, :], 0), axis=1)
    slot_of = jnp.arange(NC)[:, None] * CAP + rank
    wanted = me_col * NC + jnp.arange(NC)
    match = table[None] == wanted[:, None, None]
    incoming = jnp.sum(jnp.where(match, slot_of[None], 0), axis=(1, 2))
    return outgoing.astype(jnp.int32), incoming.astype(jnp.int32)


def row_sum(v):
    every = lax.all_to_all(jnp.broadcast_to(v[None], (NR, NC, BLK)), "row", 0, 0, tiled=True)
    return jnp.sum(every, axis=0)


def body(values, pattern, pruning, owners):
    me_row = lax.axis_index("row").astype(jnp.int32)
    me_col = lax.axis_index("col").astype(jnp.int32)
    meta = jnp.stack([me_row >> 3, (me_row >> 1) & 3, me_row & 1, me_col >> 1, me_col & 1])
    nb = ROWS // BLK
    present = lax.dynamic_slice(pattern, (me_row * nb, me_col * NC), (nb, NC))
    keep = lax.dynamic_slice(pruning, (me_row * nb, me_col * NC), (nb, NC)).reshape(nb * NC)
    outgoing, incoming = slot_tables(owners, me_col)
    m, ma, mb, p = mask_and_sum(values, present)
    p = jnp.sum(p, axis=0).reshape(NC, BLK)

    core, ring_z, ring_y = flip("t"), spread("z"), spread("y")

    def swap(x):
        return send(x, core)

    ha = send(ma, flip("xh"))
    yu = send(m, ring_y)
    mo = send(m, core)
    d = row_sum(p)
    zu = send(m, ring_z)
    fa = send(ma, flip("xl"))
    yv = send(mo, ring_y)
    zv = send(mo, ring_z)
    hb = send(mb, flip("xh"))
    fb = send(mb, flip("xl"))
    yuu = send(yu, ring_y)
    zuu = send(zu, ring_z)
    inv = jnp.broadcast_to((1.0 / d)[None], (NC, NC, BLK))
    inv = lax.all_to_all(inv, "col", 0, 0, tiled=True).reshape(NC, COLS)
    h = jnp.concatenate([ha, hb], axis=0)
    yh = send(h, ring_y)
    ho = send(h, core)
    yho = send(ho, ring_y)
    f = jnp.concatenate([fa, fb], axis=0)
    zf = send(f, ring_z)
    fo = send(f, core)
    zfo = send(fo, ring_z)
    xzz = send(zuu, flip("xl"))
    yhh = send(yh, ring_y)
    a_pieces = [m, zu, swap(zv), zuu, f, zf, swap(zfo), xzz]
    b_pieces = [m, mo, yu, yv, swap(yv), swap(yu), yuu, swap(yuu)]
    b_pieces += [h, ho, yh, yho, swap(yho), swap(yh), yhh, swap(yhh)]
    inflated, p_out = square_of(meta, keep, inv, a_pieces, b_pieces)
    norm = jnp.float32(NR * ROWS) / row_sum(p_out)
    half = (inflated * norm[:, None, :]).astype(jnp.float16)
    slots = jnp.take(half, outgoing, axis=0, mode="clip")
    arrived = lax.all_to_all(slots, "col", 0, 0, tiled=True)
    placed = jnp.take(arrived, incoming, axis=0, mode="clip").astype(jnp.float32)
    return placed.transpose(1, 0, 2).reshape(ROWS, COLS)


def solution(mesh):
    return jax.shard_map(
        body,
        mesh=mesh,
        in_specs=(P("row", "col"), P(), P(), P()),
        out_specs=P("row", "col"),
        check_vma=False,
    )
```

profile of v0, /device:TPU:0, one launch (start us, length us, event | category | flops | bytes accessed | tf_op | source)
XLA Modules:
  0.0 222.0 jit_solution(12384841808697775480)
XLA Ops:
  1.3 4.9 %shard_map.46 = (bf16[512,1024]{1,0:T(8,128)(2,1)}, bf16[256,1024]{1,0:T(8,128)(2,1)}, bf16[256,1024]{1,0:T(8,128)(2,1)}, f32[8,1024]{1,0:T(8,128)}) custom-call(s32[4,8]{1,0:T(4,128)} %dynamic_slice.13.keep_ref, f32[512,1024]{1,0:T(8,128)} %v_ref.1), custom_call_target="tpu_custom_call" | custom-call | tf_op jit(solution)/shard_map/pallas_call | solution.py:75
  6.2 3.2 %collective-permute-start.18 = (bf16[256,1024]{1,0:T(8,128)(2,1)}, bf16[256,1024]{1,0:T(8,128)(2,1)S(1)}, u32[]{:S(2)}, u32[]{:S(2)}) collective-permute-start(bf16[256,1024]{1,0:T(8,128)(2,1)} %get-tuple-element.13), channel_id=1, source_target_pairs={{0,64},{1,65},{2,66},{3,67},{4,68},{5,69},{6,70},{7,71},{8,72},{9,... | collective-permute-start | bytes 1572872 | tf_op jit(solution)/shard_map/ppermute | solution.py:46
  13.4 9.4 %collective-permute-done.18 = bf16[256,1024]{1,0:T(8,128)(2,1)S(1)} collective-permute-done((bf16[256,1024]{1,0:T(8,128)(2,1)}, bf16[256,1024]{1,0:T(8,128)(2,1)S(1)}, u32[]{:S(2)}, u32[]{:S(2)}) %collective-permute-start.18) | collective-permute-done | bytes 524320 | tf_op jit(solution)/shard_map/ppermute | solution.py:46
  24.4 9.6 %collective-permute-done.19 = bf16[256,1024]{1,0:T(8,128)(2,1)S(1)} collective-permute-done((bf16[256,1024]{1,0:T(8,128)(2,1)}, bf16[256,1024]{1,0:T(8,128)(2,1)S(1)}, u32[]{:S(2)}, u32[]{:S(2)}) %collective-permute-start.19) | collective-permute-done | bytes 524320 | tf_op jit(solution)/shard_map/ppermute | solution.py:46
  35.7 9.7 %collective-permute-done.5 = bf16[256,1024]{1,0:T(8,128)(2,1)S(1)} collective-permute-done((bf16[256,1024]{1,0:T(8,128)(2,1)}, bf16[256,1024]{1,0:T(8,128)(2,1)S(1)}, u32[]{:S(2)}, u32[]{:S(2)}) %collective-permute-start.5) | collective-permute-done | bytes 524320 | tf_op jit(solution)/shard_map/ppermute | solution.py:46
  47.1 8.5 %collective-permute-done.6 = bf16[256,1024]{1,0:T(8,128)(2,1)S(1)} collective-permute-done((bf16[256,1024]{1,0:T(8,128)(2,1)}, bf16[256,1024]{1,0:T(8,128)(2,1)S(1)}, u32[]{:S(2)}, u32[]{:S(2)}) %collective-permute-start.6) | collective-permute-done | bytes 524320 | tf_op jit(solution)/shard_map/ppermute | solution.py:46
  65.7 7.4 %collective-permute-done.7.refs_5_ = bf16[512,1024]{1,0:T(8,128)(2,1)S(1)} collective-permute-done((bf16[512,1024]{1,0:T(8,128)(2,1)S(1)}, bf16[512,1024]{1,0:T(8,128)(2,1)S(1)}, u32[]{:S(2)}, u32[]{:S(2)}) %collective-permute-start.7) | collective-permute-done | bytes 1048608 | tf_op jit(solution)/shard_map/ppermute | solution.py:46
  74.7 10.7 %collective-permute-done.16.refs_14_ = bf16[512,1024]{1,0:T(8,128)(2,1)S(1)} collective-permute-done((bf16[512,1024]{1,0:T(8,128)(2,1)S(1)}, bf16[512,1024]{1,0:T(8,128)(2,1)S(1)}, u32[]{:S(2)}, u32[]{:S(2)}) %collective-permute-start.16) | collective-permute-done | bytes 1048608 | tf_op jit(solution)/shard_map/ppermute | solution.py:46
  85.8 3.6 %collective-permute-start.24 = (bf16[512,1024]{1,0:T(8,128)(2,1)S(1)}, bf16[512,1024]{1,0:T(8,128)(2,1)S(1)}, u32[]{:S(2)}, u32[]{:S(2)}) collective-permute-start(bf16[512,1024]{1,0:T(8,128)(2,1)S(1)} %collective-permute-done.21.refs_18_), channel_id=1, source_target_pairs={{0,8},{1,9},{2,10},{3,11},{4,12},{5,13},{6,14},{7,15},{8,0},{9,1},... | collective-permute-start | bytes 3145736 | tf_op jit(solution)/shard_map/ppermute | solution.py:46
  89.3 6.3 %collective-permute-done.2 = bf16[512,1024]{1,0:T(8,128)(2,1)} collective-permute-done((bf16[512,1024]{1,0:T(8,128)(2,1)S(1)}, bf16[512,1024]{1,0:T(8,128)(2,1)}, u32[]{:S(2)}, u32[]{:S(2)}) %collective-permute-start.2) | collective-permute-done | bytes 1048608 | tf_op jit(solution)/shard_map/ppermute | solution.py:46
  95.6 2.2 %collective-permute-start.14 = (bf16[512,1024]{1,0:T(8,128)(2,1)S(1)}, bf16[512,1024]{1,0:T(8,128)(2,1)S(1)}, u32[]{:S(2)}, u32[]{:S(2)}) collective-permute-start(bf16[512,1024]{1,0:T(8,128)(2,1)S(1)} %collective-permute-done.13.refs_11_), channel_id=1, source_target_pairs={{0,8},{1,9},{2,10},{3,11},{4,12},{5,13},{6,14},{7,15},{8,0},{9,1},... | collective-permute-start | bytes 3145736 | tf_op jit(solution)/shard_map/ppermute | solution.py:46
  98.0 10.0 %collective-permute-done.22.refs_19_ = bf16[512,1024]{1,0:T(8,128)(2,1)} collective-permute-done((bf16[512,1024]{1,0:T(8,128)(2,1)S(1)}, bf16[512,1024]{1,0:T(8,128)(2,1)}, u32[]{:S(2)}, u32[]{:S(2)}) %collective-permute-start.22) | collective-permute-done | bytes 1048608 | tf_op jit(solution)/shard_map/ppermute | solution.py:46
  109.5 2.2 %collective-permute-done.9 = bf16[512,1024]{1,0:T(8,128)(2,1)} collective-permute-done((bf16[512,1024]{1,0:T(8,128)(2,1)S(1)}, bf16[512,1024]{1,0:T(8,128)(2,1)}, u32[]{:S(2)}, u32[]{:S(2)}) %collective-permute-start.9) | collective-permute-done | bytes 1048608 | tf_op jit(solution)/shard_map/ppermute | solution.py:46
  114.0 6.0 %all-to-all-start = ((f32[16,8,128]{2,1,0:T(8,128)}), f32[16,8,128]{2,1,0:T(8,128)S(1)}, u32[]{:S(2)}, u32[]{:S(2)}) async-start(f32[16,8,128]{2,1,0:T(8,128)} %broadcast_in_dim.69), calls=%async_computation | async-start | bytes 131072 | tf_op jit(solution)/shard_map/all_to_all | solution.py:187
  120.2 16.0 %all-to-all-done = f32[16,8,128]{2,1,0:T(8,128)S(1)} async-done(((f32[16,8,128]{2,1,0:T(8,128)}), f32[16,8,128]{2,1,0:T(8,128)S(1)}, u32[]{:S(2)}, u32[]{:S(2)}) %all-to-all-start) | async-done | bytes 65568 | tf_op jit(solution)/shard_map/all_to_all | solution.py:187
  136.8 3.5 %all-to-all-start.1 = ((f32[8,8,128]{2,1,0:T(8,128)}), f32[8,8,128]{2,1,0:T(8,128)S(1)}, u32[]{:S(2)}, u32[]{:S(2)}) async-start(f32[8,8,128]{2,1,0:T(8,128)} %broadcast_in_dim.70), calls=%async_computation.1 | async-start | bytes 65536 | tf_op jit(solution)/shard_map/all_to_all | solution.py:220
  142.4 4.2 %all-to-all-done.1 = f32[8,8,128]{2,1,0:T(8,128)S(1)} async-done(((f32[8,8,128]{2,1,0:T(8,128)}), f32[8,8,128]{2,1,0:T(8,128)S(1)}, u32[]{:S(2)}, u32[]{:S(2)}) %all-to-all-start.1) | async-done | bytes 32800 | tf_op jit(solution)/shard_map/all_to_all | solution.py:220
  147.3 19.4 %shard_map.47 = (f32[8,512,128]{2,1,0:T(8,128)}, f32[8,128]{1,0:T(8,128)}) custom-call(s32[5]{0:T(128)} %stack.23.meta, s32[32]{0:T(128)} %reshape.116.keep, f32[8,1024]{1,0:T(8,128)} %bitcast.16, bf16[512,1024]{1,0:T(8,128)(2,1)} %get-tuple-element.12.refs_0_.refs_8_, bf16[512,1024]{1,0:T(8,128)(2,1)} %copy-done.4, ...), custom_call_target="tpu_custom_call" | custom-call | tf_op jit(solution)/shard_map/pallas_call | solution.py:150
  168.0 4.9 %all-to-all-start.2 = ((f32[16,8,128]{2,1,0:T(8,128)}), f32[16,8,128]{2,1,0:T(8,128)S(1)}, u32[]{:S(2)}, u32[]{:S(2)}) async-start(f32[16,8,128]{2,1,0:T(8,128)} %broadcast_in_dim.71), calls=%async_computation.2 | async-start | bytes 131072 | tf_op jit(solution)/shard_map/all_to_all | solution.py:187
  172.9 7.7 %all-to-all-done.2 = f32[16,8,128]{2,1,0:T(8,128)S(1)} async-done(((f32[16,8,128]{2,1,0:T(8,128)}), f32[16,8,128]{2,1,0:T(8,128)S(1)}, u32[]{:S(2)}, u32[]{:S(2)}) %all-to-all-start.2) | async-done | bytes 65568 | tf_op jit(solution)/shard_map/all_to_all | solution.py:187
  182.4 2.7 %gather_fusion = f16[16,512,128]{2,1,0:T(8,128)(2,1)} fusion(f16[8,512,128]{2,1,0:T(8,128)(2,1)S(1)} %multiply_convert_fusion, s32[1024]{0:T(1024)S(1)} %pad_clamp_fusion.1), kind=kCustom, calls=%fused_computation | custom fusion | bytes 4194368 | tf_op jit(solution)/shard_map/jit(_take)/gather | solution.py:237
  185.1 3.6 %all-to-all-start.3 = ((f16[16,512,128]{2,1,0:T(8,128)(2,1)}), f16[16,512,128]{2,1,0:T(8,128)(2,1)S(1)}, u32[]{:S(2)}, u32[]{:S(2)}) async-start(f16[16,512,128]{2,1,0:T(8,128)(2,1)} %gather_fusion), calls=%async_computation.3 | async-start | bytes 4194304 | tf_op jit(solution)/shard_map/all_to_all | solution.py:238
  189.1 27.0 %all-to-all-done.3 = f16[16,512,128]{2,1,0:T(8,128)(2,1)S(1)} async-done(((f16[16,512,128]{2,1,0:T(8,128)(2,1)}), f16[16,512,128]{2,1,0:T(8,128)(2,1)S(1)}, u32[]{:S(2)}, u32[]{:S(2)}) %all-to-all-start.3) | async-done | bytes 2097184 | tf_op jit(solution)/shard_map/all_to_all | solution.py:238
  219.1 2.9 %copy.10 = f32[512,1024]{1,0:T(8,128)} copy(f32[512,1024]{0,1:T(8,128)} %bitcast.15) | data formatting | bytes 4194304 | tf_op jit(solution)/shard_map/reshape | solution.py:240
  (107 shorter events, 36.3 us)
Async XLA Ops:
  6.2 16.6 %collective-permute-start.18 = (bf16[256,1024]{1,0:T(8,128)(2,1)}, bf16[256,1024]{1,0:T(8,128)(2,1)S(1)}, u32[]{:S(2)}, u32[]{:S(2)}) collective-permute-start(bf16[256,1024]{1,0:T(8,128)(2,1)} %get-tuple-element.13), channel_id=1, source_target_pairs={{0,64},{1,65},{2,66},{3,67},{4,68},{5,69},{6,70},{7,71},{8,72},{9,... | collective-permute-start | bytes 1572872 | tf_op jit(solution)/shard_map/ppermute | solution.py:46
  9.4 24.6 %collective-permute-start.19 = (bf16[256,1024]{1,0:T(8,128)(2,1)}, bf16[256,1024]{1,0:T(8,128)(2,1)S(1)}, u32[]{:S(2)}, u32[]{:S(2)}) collective-permute-start(bf16[256,1024]{1,0:T(8,128)(2,1)} %get-tuple-element.14), channel_id=1, source_target_pairs={{0,64},{1,65},{2,66},{3,67},{4,68},{5,69},{6,70},{7,71},{8,72},{9,... | collective-permute-start | bytes 1572872 | tf_op jit(solution)/shard_map/ppermute | solution.py:46
  9.8 45.8 %collective-permute-start.1 = (bf16[512,1024]{1,0:T(8,128)(2,1)}, bf16[512,1024]{1,0:T(8,128)(2,1)S(1)}, u32[]{:S(2)}, u32[]{:S(2)}) collective-permute-start(bf16[512,1024]{1,0:T(8,128)(2,1)} %get-tuple-element.12.refs_0_.refs_8_), channel_id=1, source_target_pairs={{0,8},{1,9},{2,10},{3,11},{4,12},{5,13},{6,14},{7,15},{8,0},{9,1},... | collective-permute-start | bytes 3145736 | tf_op jit(solution)/shard_map/ppermute | solution.py:46
  9.8 46.4 %collective-permute-start.12 = (bf16[512,1024]{1,0:T(8,128)(2,1)}, bf16[512,1024]{1,0:T(8,128)(2,1)S(1)}, u32[]{:S(2)}, u32[]{:S(2)}) collective-permute-start(bf16[512,1024]{1,0:T(8,128)(2,1)} %get-tuple-element.12.refs_0_.refs_8_), channel_id=1, source_target_pairs={{0,16},{1,17},{2,18},{3,19},{4,20},{5,21},{6,22},{7,23},{8,56},{9,... | collective-permute-start | bytes 3145736 | tf_op jit(solution)/shard_map/ppermute | solution.py:46
  11.5 46.6 %collective-permute-start = (bf16[512,1024]{1,0:T(8,128)(2,1)}, bf16[512,1024]{1,0:T(8,128)(2,1)S(1)}, u32[]{:S(2)}, u32[]{:S(2)}) collective-permute-start(bf16[512,1024]{1,0:T(8,128)(2,1)} %get-tuple-element.12.refs_0_.refs_8_), channel_id=1, source_target_pairs={{0,2},{1,3},{2,4},{3,5},{4,6},{5,7},{6,0},{7,1},{8,14},{9,15},{10,... | collective-permute-start | bytes 3145736 | tf_op jit(solution)/shard_map/ppermute | solution.py:46
  22.8 22.7 %collective-permute-start.5 = (bf16[256,1024]{1,0:T(8,128)(2,1)}, bf16[256,1024]{1,0:T(8,128)(2,1)S(1)}, u32[]{:S(2)}, u32[]{:S(2)}) collective-permute-start(bf16[256,1024]{1,0:T(8,128)(2,1)} %get-tuple-element.13), channel_id=1, source_target_pairs={{0,1},{1,0},{2,3},{3,2},{4,5},{5,4},{6,7},{7,6},{8,9},{9,8},{10,11... | collective-permute-start | bytes 1572872 | tf_op jit(solution)/shard_map/ppermute | solution.py:46
  34.0 21.5 %collective-permute-start.6 = (bf16[256,1024]{1,0:T(8,128)(2,1)}, bf16[256,1024]{1,0:T(8,128)(2,1)S(1)}, u32[]{:S(2)}, u32[]{:S(2)}) collective-permute-start(bf16[256,1024]{1,0:T(8,128)(2,1)} %get-tuple-element.14), channel_id=1, source_target_pairs={{0,1},{1,0},{2,3},{3,2},{4,5},{5,4},{6,7},{7,6},{8,9},{9,8},{10,11... | collective-permute-start | bytes 1572872 | tf_op jit(solution)/shard_map/ppermute | solution.py:46
  56.2 16.8 %collective-permute-start.7 = (bf16[512,1024]{1,0:T(8,128)(2,1)S(1)}, bf16[512,1024]{1,0:T(8,128)(2,1)S(1)}, u32[]{:S(2)}, u32[]{:S(2)}) collective-permute-start(bf16[512,1024]{1,0:T(8,128)(2,1)S(1)} %constant_dynamic-update-slice_fusion.refs_4_), channel_id=1, source_target_pairs={{0,2},{1,3},{2,4},{3,5},{4,6},{5,7},{6,0},{7,1},{8,14},{9,15},{10,... | collective-permute-start | bytes 3145736 | tf_op jit(solution)/shard_map/ppermute | solution.py:46
  61.5 23.9 %collective-permute-start.16 = (bf16[512,1024]{1,0:T(8,128)(2,1)S(1)}, bf16[512,1024]{1,0:T(8,128)(2,1)S(1)}, u32[]{:S(2)}, u32[]{:S(2)}) collective-permute-start(bf16[512,1024]{1,0:T(8,128)(2,1)S(1)} %collective-permute-done.12.refs_10_), channel_id=1, source_target_pairs={{0,16},{1,17},{2,18},{3,19},{4,20},{5,21},{6,22},{7,23},{8,56},{9,... | collective-permute-start | bytes 3145736 | tf_op jit(solution)/shard_map/ppermute | solution.py:46
  61.8 23.9 %collective-permute-start.4 = (bf16[512,1024]{1,0:T(8,128)(2,1)S(1)}, bf16[512,1024]{1,0:T(8,128)(2,1)}, u32[]{:S(2)}, u32[]{:S(2)}) collective-permute-start(bf16[512,1024]{1,0:T(8,128)(2,1)S(1)} %collective-permute-done.refs_1_), channel_id=1, source_target_pairs={{0,2},{1,3},{2,4},{3,5},{4,6},{5,7},{6,0},{7,1},{8,14},{9,15},{10,... | collective-permute-start | bytes 3145736 | tf_op jit(solution)/shard_map/ppermute | solution.py:46
  63.8 31.9 %collective-permute-start.2 = (bf16[512,1024]{1,0:T(8,128)(2,1)S(1)}, bf16[512,1024]{1,0:T(8,128)(2,1)}, u32[]{:S(2)}, u32[]{:S(2)}) collective-permute-start(bf16[512,1024]{1,0:T(8,128)(2,1)S(1)} %collective-permute-done.1.refs_9_), channel_id=1, source_target_pairs={{0,2},{1,3},{2,4},{3,5},{4,6},{5,7},{6,0},{7,1},{8,14},{9,15},{10,... | collective-permute-start | bytes 3145736 | tf_op jit(solution)/shard_map/ppermute | solution.py:46
  73.0 22.6 %collective-permute-start.15 = (bf16[512,1024]{1,0:T(8,128)(2,1)S(1)}, bf16[512,1024]{1,0:T(8,128)(2,1)S(1)}, u32[]{:S(2)}, u32[]{:S(2)}) collective-permute-start(bf16[512,1024]{1,0:T(8,128)(2,1)S(1)} %collective-permute-done.12.refs_10_), channel_id=1, source_target_pairs={{0,8},{1,9},{2,10},{3,11},{4,12},{5,13},{6,14},{7,15},{8,0},{9,1},... | collective-permute-start | bytes 3145736 | tf_op jit(solution)/shard_map/ppermute | solution.py:46
  74.2 23.7 %collective-permute-start.25 = (bf16[512,1024]{1,0:T(8,128)(2,1)S(1)}, bf16[512,1024]{1,0:T(8,128)(2,1)}, u32[]{:S(2)}, u32[]{:S(2)}) collective-permute-start(bf16[512,1024]{1,0:T(8,128)(2,1)S(1)} %collective-permute-done.21.refs_18_), channel_id=1, source_target_pairs={{0,16},{1,17},{2,18},{3,19},{4,20},{5,21},{6,22},{7,23},{8,56},{9,... | collective-permute-start | bytes 3145736 | tf_op jit(solution)/shard_map/ppermute | solution.py:46
  85.4 22.6 %collective-permute-start.22 = (bf16[512,1024]{1,0:T(8,128)(2,1)S(1)}, bf16[512,1024]{1,0:T(8,128)(2,1)}, u32[]{:S(2)}, u32[]{:S(2)}) collective-permute-start(bf16[512,1024]{1,0:T(8,128)(2,1)S(1)} %collective-permute-done.20.refs_17_), channel_id=1, source_target_pairs={{0,16},{1,17},{2,18},{3,19},{4,20},{5,21},{6,22},{7,23},{8,56},{9,... | collective-permute-start | bytes 3145736 | tf_op jit(solution)/shard_map/ppermute | solution.py:46
  85.8 23.6 %collective-permute-start.24 = (bf16[512,1024]{1,0:T(8,128)(2,1)S(1)}, bf16[512,1024]{1,0:T(8,128)(2,1)S(1)}, u32[]{:S(2)}, u32[]{:S(2)}) collective-permute-start(bf16[512,1024]{1,0:T(8,128)(2,1)S(1)} %collective-permute-done.21.refs_18_), channel_id=1, source_target_pairs={{0,8},{1,9},{2,10},{3,11},{4,12},{5,13},{6,14},{7,15},{8,0},{9,1},... | collective-permute-start | bytes 3145736 | tf_op jit(solution)/shard_map/ppermute | solution.py:46
  95.6 16.1 %collective-permute-start.9 = (bf16[512,1024]{1,0:T(8,128)(2,1)S(1)}, bf16[512,1024]{1,0:T(8,128)(2,1)}, u32[]{:S(2)}, u32[]{:S(2)}) collective-permute-start(bf16[512,1024]{1,0:T(8,128)(2,1)S(1)} %collective-permute-done.8), channel_id=1, source_target_pairs={{0,2},{1,3},{2,4},{3,5},{4,6},{5,7},{6,0},{7,1},{8,14},{9,15},{10,... | collective-permute-start | bytes 3145736 | tf_op jit(solution)/shard_map/ppermute | solution.py:46
  95.6 16.1 %collective-permute-start.14 = (bf16[512,1024]{1,0:T(8,128)(2,1)S(1)}, bf16[512,1024]{1,0:T(8,128)(2,1)S(1)}, u32[]{:S(2)}, u32[]{:S(2)}) collective-permute-start(bf16[512,1024]{1,0:T(8,128)(2,1)S(1)} %collective-permute-done.13.refs_11_), channel_id=1, source_target_pairs={{0,8},{1,9},{2,10},{3,11},{4,12},{5,13},{6,14},{7,15},{8,0},{9,1},... | collective-permute-start | bytes 3145736 | tf_op jit(solution)/shard_map/ppermute | solution.py:46
  108.0 39.3 %collective-permute-start.11 = (bf16[512,1024]{1,0:T(8,128)(2,1)}, bf16[512,1024]{1,0:T(8,128)(2,1)}, u32[]{:S(2)}, u32[]{:S(2)}) collective-permute-start(bf16[512,1024]{1,0:T(8,128)(2,1)} %collective-permute-done.4.refs_3_), channel_id=1, source_target_pairs={{0,1},{1,0},{2,3},{3,2},{4,5},{5,4},{6,7},{7,6},{8,9},{9,8},{10,11... | collective-permute-start | bytes 3145736 | tf_op jit(solution)/shard_map/ppermute | solution.py:46
  109.4 37.8 %collective-permute-start.3 = (bf16[512,1024]{1,0:T(8,128)(2,1)}, bf16[512,1024]{1,0:T(8,128)(2,1)}, u32[]{:S(2)}, u32[]{:S(2)}) collective-permute-start(bf16[512,1024]{1,0:T(8,128)(2,1)} %collective-permute-done.2), channel_id=1, source_target_pairs={{0,8},{1,9},{2,10},{3,11},{4,12},{5,13},{6,14},{7,15},{8,0},{9,1},... | collective-permute-start | bytes 3145736 | tf_op jit(solution)/shard_map/ppermute | solution.py:46
  111.7 35.5 %collective-permute-start.26 = (bf16[512,1024]{1,0:T(8,128)(2,1)}, bf16[512,1024]{1,0:T(8,128)(2,1)}, u32[]{:S(2)}, u32[]{:S(2)}) collective-permute-start(bf16[512,1024]{1,0:T(8,128)(2,1)} %collective-permute-done.25.refs_22_), channel_id=1, source_target_pairs={{0,8},{1,9},{2,10},{3,11},{4,12},{5,13},{6,14},{7,15},{8,0},{9,1},... | collective-permute-start | bytes 3145736 | tf_op jit(solution)/shard_map/ppermute | solution.py:46
  111.8 35.5 %collective-permute-start.23 = (bf16[512,1024]{1,0:T(8,128)(2,1)}, bf16[512,1024]{1,0:T(8,128)(2,1)}, u32[]{:S(2)}, u32[]{:S(2)}) collective-permute-start(bf16[512,1024]{1,0:T(8,128)(2,1)} %collective-permute-done.22.refs_19_), channel_id=1, source_target_pairs={{0,8},{1,9},{2,10},{3,11},{4,12},{5,13},{6,14},{7,15},{8,0},{9,1},... | collective-permute-start | bytes 3145736 | tf_op jit(solution)/shard_map/ppermute | solution.py:46
  112.3 34.9 %collective-permute-start.10 = (bf16[512,1024]{1,0:T(8,128)(2,1)}, bf16[512,1024]{1,0:T(8,128)(2,1)}, u32[]{:S(2)}, u32[]{:S(2)}) collective-permute-start(bf16[512,1024]{1,0:T(8,128)(2,1)} %collective-permute-done.9), channel_id=1, source_target_pairs={{0,8},{1,9},{2,10},{3,11},{4,12},{5,13},{6,14},{7,15},{8,0},{9,1},... | collective-permute-start | bytes 3145736 | tf_op jit(solution)/shard_map/ppermute | solution.py:46
  114.0 22.2 %all-to-all-start = ((f32[16,8,128]{2,1,0:T(8,128)}), f32[16,8,128]{2,1,0:T(8,128)S(1)}, u32[]{:S(2)}, u32[]{:S(2)}) async-start(f32[16,8,128]{2,1,0:T(8,128)} %broadcast_in_dim.69), calls=%async_computation | async-start | bytes 131072 | tf_op jit(solution)/shard_map/all_to_all | solution.py:187
  185.1 31.0 %all-to-all-start.3 = ((f16[16,512,128]{2,1,0:T(8,128)(2,1)}), f16[16,512,128]{2,1,0:T(8,128)(2,1)S(1)}, u32[]{:S(2)}, u32[]{:S(2)}) async-start(f16[16,512,128]{2,1,0:T(8,128)(2,1)} %gather_fusion), calls=%async_computation.3 | async-start | bytes 4194304 | tf_op jit(solution)/shard_map/all_to_all | solution.py:238
  (23 other events, 874.7 us)
where the time goes:
time: 223 us; the launch traced here: 222 us
  waiting for transfers between devices  131 us (59%)
  starting transfers between devices  47.3 us (21%)
  Pallas kernels  24.3 us (11%)
  local copies, waits for them, and re-layouts  16 us (7%)
  other arithmetic  2.6 us (1%)
    ppermute x27, waiting for transfers between devices, send(): return lax.ppermute(x, AXES, pairs)  76.6 us
    ppermute x27, starting transfers between devices, send(): return lax.ppermute(x, AXES, pairs)  29.3 us
    all_to_all x1, waiting for transfers between devices, body(): arrived = lax.all_to_all(slots, 'col', 0, 0, tiled=True)  27 us
    all_to_all x2, waiting for transfers between devices, row_sum(): lax.all_to_all(jnp.broadcast_to(v[None], (NR, NC, BLK)), 'row', 0, 0, til...  23.6 us
    pallas_call x1, Pallas kernels, square_of(): pl.pallas_call(square_kernel, in_specs=[smem, smem, pl.BlockSpec(memory_s...  19.4 us
    all_to_all x2, starting transfers between devices, row_sum(): lax.all_to_all(jnp.broadcast_to(v[None], (NR, NC, BLK)), 'row', 0, 0, til...  10.9 us
    pallas_call x1, Pallas kernels, mask_and_sum(): pl.pallas_call(mask_kernel, grid_spec=pltpu.PrefetchScalarGridSpec(num_sc...  4.89 us
    reshape x2, local copies, waits for them, and re-layouts, body(): return placed.transpose(1, 0, 2).reshape(ROWS, COLS)  4.72 us
  transfers between devices with their start and end apart: 31, of which 15 were waited for; matrix products, arithmetic and copies ran while one was open for 2% of the time, Pallas kernels for 0%

commit v1 on v0

--- a/solution.py
+++ b/solution.py
@@ -12,6 +12,8 @@
 NC = 8
 NR = 16
 CAP = 2
+EARLY_LIMIT = 4 << 20
+LATE_LIMIT = 19 << 20
 AXES = ("row", "col")
 
 
@@ -38,6 +40,15 @@
     for i in range(NR * NC):
         d = decode(i)
         d[axis] = (d[axis] + (1 if d["t"] == 0 else -1)) % 4
+        out.append((i, encode(d)))
+    return out
+
+
+def ring_xor(bit):
+    out = []
+    for i in range(NR * NC):
+        d = decode(i)
+        d["y"] ^= bit
         out.append((i, encode(d)))
     return out
 
@@ -94,43 +105,88 @@
     )(keep, values)
 
 
-def square_kernel(meta, keep, inv_ref, *refs):
-    a_refs, b_refs = refs[:8], refs[8:24]
-    h_ref, p_ref = refs[24:26]
-    a_buf, b_buf, acc, a_sem, b_sem = refs[26:]
+def early_kernel(meta, keep, outgoing, incoming, inv_ref, *refs):
+    del keep, outgoing, incoming
+    a_refs, b_refs = refs[:4], refs[4:12]
+    a_buf, b_buf, acc, sem = refs[12:]
     xh, y, t, z, xl = (meta[i] for i in range(5))
-    step = 2 * t - 1
-    copies_a = []
-    for i in range(8):
-        dz = (0, step, -step, 2)[i % 4]
-        c = ((z + dz) & 3) * 2 + (xl ^ (i // 4))
-        copies_a.append(pltpu.make_async_copy(a_refs[i], a_buf.at[c], a_sem.at[i]))
-    lo, hi = pl.multiple_of(t * ROWS, ROWS), pl.multiple_of((1 - t) * ROWS, ROWS)
-    order = []
-    for i in range(8):
-        dy = (0, step, -step, 2)[i % 4]
-        c = (xh ^ (i // 4)) * 4 + ((y + dy) & 3)
-        group = []
-        for k, at in ((2 * i, lo), (2 * i + 1, hi)):
-            dst = b_buf.at[c, pl.ds(at, ROWS)]
-            group.append(pltpu.make_async_copy(b_refs[k], dst, b_sem.at[k]))
-        order.append((c, group))
-    for copy in copies_a:
+    copies = panel_copies(t, z, y, [[r] for r in a_refs], b_refs, a_buf, b_buf, sem)
+    for copy in copies[0] + copies[1]:
         copy.start()
-    for _, group in order:
-        for copy in group:
-            copy.start()
-    for copy in copies_a:
+    for copy in copies[0] + copies[1]:
         copy.wait()
-    for n, (c, group) in enumerate(order):
-        for copy in group:
-            copy.wait()
-        a = (a_buf[c].astype(jnp.float32) * inv_ref[pl.ds(c, 1), :]).astype(jnp.bfloat16)
-        part = jnp.dot(a, b_buf[c], preferred_element_type=jnp.float32)
-        if n == 0:
+    for k in range(2):
+        part = block_product(inv_ref, a_buf, b_buf, xh, xl + 2 * k)
+        if k == 0:
             acc[...] = part
         else:
             acc[...] += part
+
+
+def panel_copies(t, z, y, a_pieces, b_pieces, a_buf, b_buf, sem):
+    step = 2 * t - 1
+    lo, hi = pl.multiple_of(t * ROWS, ROWS), pl.multiple_of((1 - t) * ROWS, ROWS)
+    first, second = [], []
+    for i in range(4):
+        d = (0, step, -step, 2)[i]
+        at = 0
+        for ref in a_pieces[i]:
+            rows = ref.shape[0]
+            n = len(first)
+            dst = a_buf.at[(z + d) & 3, pl.ds(at, rows)]
+            first.append(pltpu.make_async_copy(ref, dst, sem.at[n]))
+            at += rows
+        for k, at in ((2 * i, lo), (2 * i + 1, hi)):
+            dst = b_buf.at[(y + d) & 3, pl.ds(at, ROWS)]
+            second.append(pltpu.make_async_copy(b_pieces[k], dst, sem.at[8 + k]))
+    return first, second
+
+
+def block_product(inv_ref, a_buf, b_buf, xh, y):
+    scale = inv_ref[pl.ds(xh * 4 + y, 1), :]
+    a = (a_buf[xh * 2 + (y >> 1)].astype(jnp.float32) * scale).astype(jnp.bfloat16)
+    return jnp.dot(a, b_buf[y], preferred_element_type=jnp.float32)
+
+
+def early_product(meta, tables, inv, a_pieces, b_pieces):
+    anywhere = pl.BlockSpec(memory_space=pltpu.HBM)
+    smem = pl.BlockSpec(memory_space=pltpu.SMEM)
+    vmem = pl.BlockSpec(memory_space=pltpu.VMEM)
+    out = pl.pallas_call(
+        early_kernel,
+        in_specs=[smem] * 4 + [vmem] + [anywhere] * 12,
+        out_specs=[vmem] * 3,
+        out_shape=[
+            jax.ShapeDtypeStruct((4, ROWS, COLS), jnp.bfloat16),
+            jax.ShapeDtypeStruct((4, 2 * ROWS, COLS), jnp.bfloat16),
+            jax.ShapeDtypeStruct((ROWS, COLS), jnp.float32),
+        ],
+        scratch_shapes=[pltpu.SemaphoreType.DMA((16,))],
+        compiler_params=pltpu.CompilerParams(vmem_limit_bytes=EARLY_LIMIT),
+    )(meta, *tables, inv, *a_pieces, *b_pieces)
+    return [pltpu.with_memory_space_constraint(x, pltpu.VMEM) for x in out]
+
+
+def late_kernel(meta, keep, inv_ref, ae_ref, be_ref, part_ref, *refs):
+    a_refs, b_refs = refs[:7], refs[7:15]
+    h_ref, p_ref = refs[15:17]
+    a_buf, b_buf, acc, sem = refs[17:]
+    xh, y, t, z, xl = (meta[i] for i in range(5))
+    pieces = [a_refs[0:2], a_refs[2:4], a_refs[4:6], a_refs[6:7]]
+    first, second = panel_copies(t, z, y, pieces, b_refs, a_buf, b_buf, sem)
+    for copy in first + second:
+        copy.start()
+    for copy in first:
+        copy.wait()
+    acc[...] = part_ref[...]
+    for k in range(2):
+        acc[...] += block_product(inv_ref, a_buf, be_ref, xh, (1 - xl) + 2 * k)
+    for copy in second:
+        copy.wait()
+    for k in range(2):
+        acc[...] += block_product(inv_ref, ae_ref, b_buf, 1 - xh, xl + 2 * k)
+    for k in range(2):
+        acc[...] += block_product(inv_ref, a_buf, b_buf, 1 - xh, (1 - xl) + 2 * k)
     scale = inv_ref[pl.ds(z * 2 + xl, 1), :]
     for j in range(NC):
         sl = pl.ds(j * BLK, BLK)
@@ -141,28 +197,54 @@
             g = jnp.where(keep[i * NC + j] != 0, g * g, jnp.zeros_like(g))
             h_ref[j, rows] = g
             total += jnp.sum(g.reshape(BLK // 8, 8, BLK), axis=0)
-        p_ref[pl.ds(j, 1), :] = jnp.sum(total, axis=0, keepdims=True)
-
-
-def square_of(meta, keep, inv, a_pieces, b_pieces):
-    anywhere = pl.BlockSpec(memory_space=pl.ANY)
+        total = jnp.sum(total, axis=0, keepdims=True)
+        p_ref[pl.ds(j, 1), :] = total
+        r = jnp.where(total > 0, 1.0 / total, jnp.zeros_like(total))
+        h_ref[j] = h_ref[j] * r * jnp.float32(ROWS)
+
+
+def late_product(meta, keep, inv, early, a_pieces, b_pieces):
+    anywhere = pl.BlockSpec(memory_space=pltpu.HBM)
     smem = pl.BlockSpec(memory_space=pltpu.SMEM)
+    vmem = pl.BlockSpec(memory_space=pltpu.VMEM)
     return pl.pallas_call(
-        square_kernel,
-        in_specs=[smem, smem, pl.BlockSpec(memory_space=pltpu.VMEM)] + [anywhere] * 24,
-        out_specs=[pl.BlockSpec(memory_space=pltpu.VMEM)] * 2,
+        late_kernel,
+        in_specs=[smem, smem] + [vmem] * 4 + [anywhere] * 15,
+        out_specs=[vmem] * 2,
         out_shape=[
             jax.ShapeDtypeStruct((NC, ROWS, BLK), jnp.float32),
             jax.ShapeDtypeStruct((NC, BLK), jnp.float32),
         ],
         scratch_shapes=[
-            pltpu.VMEM((NC, ROWS, COLS), jnp.bfloat16),
-            pltpu.VMEM((NC, 2 * ROWS, COLS), jnp.bfloat16),
+            pltpu.VMEM((4, ROWS, COLS), jnp.bfloat16),
+            pltpu.VMEM((4, 2 * ROWS, COLS), jnp.bfloat16),
             pltpu.VMEM((ROWS, COLS), jnp.float32),
-            pltpu.SemaphoreType.DMA((8,)),
             pltpu.SemaphoreType.DMA((16,)),
         ],
-    )(meta, keep, inv, *a_pieces, *b_pieces)
+        compiler_params=pltpu.CompilerParams(vmem_limit_bytes=LATE_LIMIT),
+    )(meta, keep, inv, *early, *a_pieces, *b_pieces)
+
+
+def columns_kernel(x_ref, o_ref, sem):
+    copies = []
+    for j in range(NC):
+        dst = o_ref.at[:, pl.ds(j * BLK, BLK)]
+        copies.append(pltpu.make_async_copy(x_ref.at[j], dst, sem.at[j]))
+    for copy in copies:
+        copy.start()
+    for copy in copies:
+        copy.wait()
+
+
+def side_by_side(blocks):
+    return pl.pallas_call(
+        columns_kernel,
+        in_specs=[pl.BlockSpec(memory_space=pltpu.VMEM)],
+        out_specs=pl.BlockSpec(memory_space=pltpu.HBM),
+        out_shape=jax.ShapeDtypeStruct((ROWS, COLS), jnp.float32),
+        scratch_shapes=[pltpu.SemaphoreType.DMA((NC,))],
+        compiler_params=pltpu.CompilerParams(vmem_limit_bytes=EARLY_LIMIT),
+    )(pltpu.with_memory_space_constraint(blocks, pltpu.VMEM))
 
 
 def slot_tables(owners, me_col):
@@ -195,7 +277,6 @@
     nb = ROWS // BLK
     present = lax.dynamic_slice(pattern, (me_row * nb, me_col * NC), (nb, NC))
     keep = lax.dynamic_slice(pruning, (me_row * nb, me_col * NC), (nb, NC)).reshape(nb * NC)
-    outgoing, incoming = slot_tables(owners, me_col)
     m, ma, mb, p = mask_and_sum(values, present)
     p = jnp.sum(p, axis=0).reshape(NC, BLK)
 
@@ -204,40 +285,53 @@
     def swap(x):
         return send(x, core)
 
-    ha = send(ma, flip("xh"))
+    outgoing, incoming = slot_tables(owners, me_col)
+    h = send(m, flip("xh"))
     yu = send(m, ring_y)
     mo = send(m, core)
     d = row_sum(p)
     zu = send(m, ring_z)
-    fa = send(ma, flip("xl"))
     yv = send(mo, ring_y)
     zv = send(mo, ring_z)
-    hb = send(mb, flip("xh"))
+    fa = send(ma, flip("xl"))
     fb = send(mb, flip("xl"))
     yuu = send(yu, ring_y)
     zuu = send(zu, ring_z)
     inv = jnp.broadcast_to((1.0 / d)[None], (NC, NC, BLK))
     inv = lax.all_to_all(inv, "col", 0, 0, tiled=True).reshape(NC, COLS)
-    h = jnp.concatenate([ha, hb], axis=0)
+    ho = send(h, core)
     yh = send(h, ring_y)
-    ho = send(h, core)
     yho = send(ho, ring_y)
-    f = jnp.concatenate([fa, fb], axis=0)
-    zf = send(f, ring_z)
-    fo = send(f, core)
-    zfo = send(fo, ring_z)
+    foa = send(fa, core)
+    zfa = send(fa, ring_z)
+    zfoa = send(foa, ring_z)
+    fob = send(fb, core)
+    zfb = send(fb, ring_z)
+    zfob = send(fob, ring_z)
     xzz = send(zuu, flip("xl"))
     yhh = send(yh, ring_y)
-    a_pieces = [m, zu, swap(zv), zuu, f, zf, swap(zfo), xzz]
-    b_pieces = [m, mo, yu, yv, swap(yv), swap(yu), yuu, swap(yuu)]
-    b_pieces += [h, ho, yh, yho, swap(yho), swap(yh), yhh, swap(yhh)]
-    inflated, p_out = square_of(meta, keep, inv, a_pieces, b_pieces)
-    norm = jnp.float32(NR * ROWS) / row_sum(p_out)
-    half = (inflated * norm[:, None, :]).astype(jnp.float16)
-    slots = jnp.take(half, outgoing, axis=0, mode="clip")
+    early = early_product(
+        meta, (keep, outgoing, incoming), inv,
+        [m, zu, swap(zv), zuu],
+        [m, mo, yu, yv, swap(yv), swap(yu), yuu, swap(yuu)],
+    )
+    shares, p_out = late_product(
+        meta, keep, inv, early,
+        [fa, fb, zfa, zfb, swap(zfoa), swap(zfob), xzz],
+        [h, ho, yh, yho, swap(yho), swap(yh), yhh, swap(yhh)],
+    )
+    sums = jnp.take(p_out, outgoing, axis=0, mode="clip")
+    sums = lax.all_to_all(sums, "col", 0, 0, tiled=True)
+    slots = jnp.take(shares.astype(jnp.float16), outgoing, axis=0, mode="clip")
     arrived = lax.all_to_all(slots, "col", 0, 0, tiled=True)
-    placed = jnp.take(arrived, incoming, axis=0, mode="clip").astype(jnp.float32)
-    return placed.transpose(1, 0, 2).reshape(ROWS, COLS)
+    sums = jnp.take(sums, incoming, axis=0, mode="clip")
+    total = sums + send(sums, core)
+    total = total + send(total, ring_xor(1))
+    total = total + send(total, ring_xor(2))
+    total = total + send(total, flip("xh"))
+    weight = sums / total * jnp.float32(NR)
+    placed = jnp.take(arrived, incoming, axis=0, mode="clip")
+    return side_by_side(placed.astype(jnp.float32) * weight[:, None, :])
 
 
 def solution(mesh):

time: 223 us -> 210 us (0.942)
  waiting for transfers between devices: 131 us -> 113 us
  starting transfers between devices: 47.3 us -> 53 us
  local copies, waits for them, and re-layouts: 16 us -> 18.7 us
  Pallas kernels: 24.3 us -> 21.8 us
    all_to_all x1, waiting for transfers between devices: 27 us -> 0.01 us  [body(): arrived = lax.all_to_all(slots, 'col', 0, 0, tiled=True)]
    ppermute x27 -> x34, waiting for transfers between devices: 76.6 us -> 103 us  [send(): return lax.ppermute(x, AXES, pairs)]
    all_to_all x2 -> x1, waiting for transfers between devices: 23.6 us -> 0.17 us  [row_sum(): lax.all_to_all(jnp.broadcast_to(v[None], (NR, NC, BLK)), 'row', 0, 0, til...]
    unnamed x35 -> x37, local copies, waits for them, and re-layouts: 1.59 us -> 9.69 us
    ppermute x27 -> x34, starting transfers between devices: 29.3 us -> 36.6 us  [send(): return lax.ppermute(x, AXES, pairs)]
    all_to_all x2 -> x1, starting transfers between devices: 10.9 us -> 5.16 us  [row_sum(): lax.all_to_all(jnp.broadcast_to(v[None], (NR, NC, BLK)), 'row', 0, 0, til...]
    reshape x2 -> x0, local copies, waits for them, and re-layouts: 4.72 us -> none  [body(): return placed.transpose(1, 0, 2).reshape(ROWS, COLS)]
    all_to_all x0 -> x1, starting transfers between devices: none -> 3.32 us  [body(): sums = lax.all_to_all(sums, 'col', 0, 0, tiled=True)]
  transfers between devices with their start and end apart: 31 -> 38, of which waited for: 15 -> 18; matrix products, arithmetic and copies ran while one was open for 2% -> 3% of each run, Pallas kernels for 0% -> 3%
where the time goes in v1:
time: 210 us; the launch traced here: 209 us
  waiting for transfers between devices  113 us (54%)
  starting transfers between devices  53 us (25%)
  Pallas kernels  21.8 us (10%)
  local copies, waits for them, and re-layouts  18.7 us (9%)
    ppermute x34, waiting for transfers between devices, send(): return lax.ppermute(x, AXES, pairs)  103 us
    ppermute x34, starting transfers between devices, send(): return lax.ppermute(x, AXES, pairs)  36.6 us
    unnamed x37, local copies, waits for them, and re-layouts  9.69 us
    pallas_call x1, Pallas kernels, late_product(): pl.pallas_call(late_kernel, in_specs=[smem, smem] + [vmem] * 4 + [anywher...  9.45 us
    all_to_all x1, waiting for transfers between devices, body(): inv = lax.all_to_all(inv, 'col', 0, 0, tiled=True).reshape(NC, COLS)  6.72 us
    pallas_call x1, Pallas kernels, early_product(): pl.pallas_call(early_kernel, in_specs=[smem] * 4 + [vmem] + [anywhere] *...  6.04 us
    all_to_all x1, starting transfers between devices, row_sum(): lax.all_to_all(jnp.broadcast_to(v[None], (NR, NC, BLK)), 'row', 0, 0, til...  5.16 us
    pallas_call x1, Pallas kernels, mask_and_sum(): pl.pallas_call(mask_kernel, grid_spec=pltpu.PrefetchScalarGridSpec(num_sc...  4.88 us
  transfers between devices with their start and end apart: 38, of which 18 were waited for; matrix products, arithmetic and copies ran while one was open for 3% of the time, Pallas kernels for 3%

profile of v1, /device:TPU:0, one launch (start us, length us, event | category | flops | bytes accessed | tf_op | source)
XLA Modules:
  0.0 208.7 jit_solution(3280306287058627319)
XLA Ops:
  1.4 4.9 %shard_map.46 = (bf16[512,1024]{1,0:T(8,128)(2,1)}, bf16[256,1024]{1,0:T(8,128)(2,1)}, bf16[256,1024]{1,0:T(8,128)(2,1)}, f32[8,1024]{1,0:T(8,128)}) custom-call(s32[4,8]{1,0:T(4,128)} %dynamic_slice.13.keep_ref, f32[512,1024]{1,0:T(8,128)} %v_ref.1), custom_call_target="tpu_custom_call" | custom-call | tf_op jit(solution)/shard_map/pallas_call | solution.py:86
  12.1 2.7 %collective-permute-start.22 = (bf16[512,1024]{1,0:T(8,128)(2,1)}, bf16[512,1024]{1,0:T(8,128)(2,1)S(1)}, u32[]{:S(2)}, u32[]{:S(2)}) collective-permute-start(bf16[512,1024]{1,0:T(8,128)(2,1)} %get-tuple-element.15.refs_0_.refs_4_), channel_id=1, source_target_pairs={{0,64},{1,65},{2,66},{3,67},{4,68},{5,69},{6,70},{7,71},{8,72},{9,... | collective-permute-start | bytes 3145736 | tf_op jit(solution)/shard_map/ppermute | solution.py:57
  14.9 6.5 %collective-permute-done.11.refs_0_ = bf16[256,1024]{1,0:T(8,128)(2,1)S(1)} collective-permute-done((bf16[256,1024]{1,0:T(8,128)(2,1)}, bf16[256,1024]{1,0:T(8,128)(2,1)S(1)}, u32[]{:S(2)}, u32[]{:S(2)}) %collective-permute-start.11) | collective-permute-done | bytes 524320 | tf_op jit(solution)/shard_map/ppermute | solution.py:57
  22.9 30.8 %collective-permute-done.12.refs_1_ = bf16[256,1024]{1,0:T(8,128)(2,1)S(1)} collective-permute-done((bf16[256,1024]{1,0:T(8,128)(2,1)}, bf16[256,1024]{1,0:T(8,128)(2,1)S(1)}, u32[]{:S(2)}, u32[]{:S(2)}) %collective-permute-start.12) | collective-permute-done | bytes 524320 | tf_op jit(solution)/shard_map/ppermute | solution.py:57
  54.3 2.2 %collective-permute-start.13 = (bf16[256,1024]{1,0:T(8,128)(2,1)S(1)}, bf16[256,1024]{1,0:T(8,128)(2,1)S(1)}, u32[]{:S(2)}, u32[]{:S(2)}) collective-permute-start(bf16[256,1024]{1,0:T(8,128)(2,1)S(1)} %collective-permute-done.11.refs_0_), channel_id=1, source_target_pairs={{0,2},{1,3},{2,4},{3,5},{4,6},{5,7},{6,0},{7,1},{8,14},{9,15},{10,... | collective-permute-start | bytes 1572872 | tf_op jit(solution)/shard_map/ppermute | solution.py:57
  66.5 4.8 %collective-permute-done.14.refs_3_ = bf16[256,1024]{1,0:T(8,128)(2,1)S(1)} collective-permute-done((bf16[256,1024]{1,0:T(8,128)(2,1)S(1)}, bf16[256,1024]{1,0:T(8,128)(2,1)S(1)}, u32[]{:S(2)}, u32[]{:S(2)}) %collective-permute-start.14) | collective-permute-done | bytes 524320 | tf_op jit(solution)/shard_map/ppermute | solution.py:57
  72.3 4.6 %collective-permute-done.16 = bf16[256,1024]{1,0:T(8,128)(2,1)S(1)} collective-permute-done((bf16[256,1024]{1,0:T(8,128)(2,1)S(1)}, bf16[256,1024]{1,0:T(8,128)(2,1)S(1)}, u32[]{:S(2)}, u32[]{:S(2)}) %collective-permute-start.16) | collective-permute-done | bytes 524320 | tf_op jit(solution)/shard_map/ppermute | solution.py:57
  77.1 5.5 %collective-permute-done.19 = bf16[256,1024]{1,0:T(8,128)(2,1)} collective-permute-done((bf16[256,1024]{1,0:T(8,128)(2,1)S(1)}, bf16[256,1024]{1,0:T(8,128)(2,1)}, u32[]{:S(2)}, u32[]{:S(2)}) %collective-permute-start.19) | collective-permute-done | bytes 524320 | tf_op jit(solution)/shard_map/ppermute | solution.py:57
  85.8 8.2 %collective-permute-done.2 = bf16[512,1024]{1,0:T(8,128)(2,1)} collective-permute-done((bf16[512,1024]{1,0:T(8,128)(2,1)S(1)}, bf16[512,1024]{1,0:T(8,128)(2,1)}, u32[]{:S(2)}, u32[]{:S(2)}) %collective-permute-start.2) | collective-permute-done | bytes 1048608 | tf_op jit(solution)/shard_map/ppermute | solution.py:57
  93.9 11.1 %collective-permute-done.4.refs_3_ = bf16[512,1024]{1,0:T(8,128)(2,1)S(1)} collective-permute-done((bf16[512,1024]{1,0:T(8,128)(2,1)S(1)}, bf16[512,1024]{1,0:T(8,128)(2,1)S(1)}, u32[]{:S(2)}, u32[]{:S(2)}) %collective-permute-start.4) | collective-permute-done | bytes 1048608 | tf_op jit(solution)/shard_map/ppermute | solution.py:57
  113.9 5.2 %all-to-all-start = ((f32[16,8,128]{2,1,0:T(8,128)}), f32[16,8,128]{2,1,0:T(8,128)S(1)}, u32[]{:S(2)}, u32[]{:S(2)}) async-start(f32[16,8,128]{2,1,0:T(8,128)} %broadcast_in_dim.67), calls=%async_computation | async-start | bytes 131072 | tf_op jit(solution)/shard_map/all_to_all | solution.py:269
  121.5 11.8 %collective-permute-done.25.refs_10_ = bf16[512,1024]{1,0:T(8,128)(2,1)} collective-permute-done((bf16[512,1024]{1,0:T(8,128)(2,1)}, bf16[512,1024]{1,0:T(8,128)(2,1)}, u32[]{:S(2)}, u32[]{:S(2)}) %collective-permute-start.25) | collective-permute-done | bytes 1048608 | tf_op jit(solution)/shard_map/ppermute | solution.py:57
  135.0 4.3 %all-to-all-start.1 = ((f32[8,8,128]{2,1,0:T(8,128)}), f32[8,8,128]{2,1,0:T(8,128)S(1)}, u32[]{:S(2)}, u32[]{:S(2)}) async-start(f32[8,8,128]{2,1,0:T(8,128)} %broadcast_in_dim.68), calls=%async_computation.1 | async-start | bytes 65536 | tf_op jit(solution)/shard_map/all_to_all | solution.py:301
  140.3 6.7 %all-to-all-done.1 = f32[8,8,128]{2,1,0:T(8,128)S(1)} async-done(((f32[8,8,128]{2,1,0:T(8,128)}), f32[8,8,128]{2,1,0:T(8,128)S(1)}, u32[]{:S(2)}, u32[]{:S(2)}) %all-to-all-start.1) | async-done | bytes 32800 | tf_op jit(solution)/shard_map/all_to_all | solution.py:301
  150.7 6.0 %shard_map.47 = (bf16[4,512,1024]{2,1,0:T(8,128)(2,1)S(1)}, bf16[4,1024,1024]{2,1,0:T(8,128)(2,1)S(1)}, f32[512,1024]{1,0:T(8,128)S(1)}) custom-call(s32[5]{0:T(128)S(1)} %stack.23.meta, s32[32]{0:T(128)S(1)} %reshape.109.keep, s32[16]{0:T(128)S(1)} %select_reduce_fusion.2.outgoing, s32[8]{0:T(128)S(1)} %select_reduce_fusion.incoming, ...), custom_call_target="tpu_custom_call" | custom-call | tf_op jit(solution)/shard_map/pallas_call | solution.py:155
  156.9 9.5 %shard_map.48 = (f32[8,512,128]{2,1,0:T(8,128)S(1)}, f32[8,128]{1,0:T(8,128)S(1)}) custom-call(s32[5]{0:T(128)S(1)} %stack.23.meta, s32[32]{0:T(128)S(1)} %reshape.109.keep, f32[8,1024]{1,0:T(8,128)S(1)} %bitcast.15, bf16[4,512,1024]{2,1,0:T(8,128)(2,1)S(1)} %get-tuple-element.16.ae_ref, bf16[4,1024,1024]{2,1,0:T(8,128)(2,1)S(1)} %get-tuple-element.17.be_ref, ...), custom_call_target="tpu_custom_call" | custom-call | tf_op jit(solution)/shard_map/pallas_call | solution.py:210
  167.5 3.3 %all-to-all-start.3 = ((f32[8,2,128]{2,1,0:T(2,128)}), f32[8,2,128]{2,1,0:T(2,128)S(1)}, u32[]{:S(2)}, u32[]{:S(2)}) async-start(f32[8,2,128]{2,1,0:T(2,128)} %bitcast.7), calls=%async_computation.3 | async-start | bytes 16384 | tf_op jit(solution)/shard_map/all_to_all | solution.py:324
  171.0 2.7 %gather_fusion = f16[16,512,128]{2,1,0:T(8,128)(2,1)} fusion(f16[8,512,128]{2,1,0:T(8,128)(2,1)S(1)} %convert_element_type.6, s32[1024]{0:T(1024)S(1)} %pad_clamp_fusion.1), kind=kCustom, calls=%fused_computation | custom fusion | bytes 4194368 | tf_op jit(solution)/shard_map/jit(_take)/gather | solution.py:325
  173.6 3.3 %all-to-all-done.3 = f32[8,2,128]{2,1,0:T(2,128)S(1)} async-done(((f32[8,2,128]{2,1,0:T(2,128)}), f32[8,2,128]{2,1,0:T(2,128)S(1)}, u32[]{:S(2)}, u32[]{:S(2)}) %all-to-all-start.3) | async-done | bytes 8224 | tf_op jit(solution)/shard_map/all_to_all | solution.py:324
  176.9 3.6 %all-to-all-start.2 = ((f16[16,512,128]{2,1,0:T(8,128)(2,1)}), f16[16,512,128]{2,1,0:T(8,128)(2,1)S(1)}, u32[]{:S(2)}, u32[]{:S(2)}) async-start(f16[16,512,128]{2,1,0:T(8,128)(2,1)} %gather_fusion), calls=%async_computation.2 | async-start | bytes 4194304 | tf_op jit(solution)/shard_map/all_to_all | solution.py:326
  182.4 1.9 collective-permute-start.31
  186.0 3.4 %collective-permute-start.32 = (f32[8,128]{1,0:T(8,128)S(1)}, f32[8,128]{1,0:T(8,128)S(1)}, u32[]{:S(2)}, u32[]{:S(2)}) collective-permute-start(f32[8,128]{1,0:T(8,128)S(1)} %add.67), channel_id=1, source_target_pairs={{0,32},{1,33},{2,34},{3,35},{4,36},{5,37},{6,38},{7,39},{8,40},{9,... | collective-permute-start | bytes 12296 | tf_op jit(solution)/shard_map/ppermute | solution.py:57
  191.1 3.5 %collective-permute-start.33 = (f32[8,128]{1,0:T(8,128)S(1)}, f32[8,128]{1,0:T(8,128)S(1)}, u32[]{:S(2)}, u32[]{:S(2)}) collective-permute-start(f32[8,128]{1,0:T(8,128)S(1)} %add.68), channel_id=1, source_target_pairs={{0,64},{1,65},{2,66},{3,67},{4,68},{5,69},{6,70},{7,71},{8,72},{9,... | collective-permute-start | bytes 12296 | tf_op jit(solution)/shard_map/ppermute | solution.py:57
  194.6 11.4 %collective-permute-done.33 = f32[8,128]{1,0:T(8,128)S(1)} collective-permute-done((f32[8,128]{1,0:T(8,128)S(1)}, f32[8,128]{1,0:T(8,128)S(1)}, u32[]{:S(2)}, u32[]{:S(2)}) %collective-permute-start.33) | collective-permute-done | bytes 4128 | tf_op jit(solution)/shard_map/ppermute | solution.py:57
  (124 shorter events, 50.3 us)
Async XLA Ops:
  7.9 45.9 %collective-permute-start.5 = (bf16[512,1024]{1,0:T(8,128)(2,1)}, bf16[512,1024]{1,0:T(8,128)(2,1)S(1)}, u32[]{:S(2)}, u32[]{:S(2)}) collective-permute-start(bf16[512,1024]{1,0:T(8,128)(2,1)} %get-tuple-element.15.refs_0_.refs_4_), channel_id=1, source_target_pairs={{0,16},{1,17},{2,18},{3,19},{4,20},{5,21},{6,22},{7,23},{8,56},{9,... | collective-permute-start | bytes 3145736 | tf_op jit(solution)/shard_map/ppermute | solution.py:57
  9.5 44.8 %collective-permute-start.1 = (bf16[512,1024]{1,0:T(8,128)(2,1)}, bf16[512,1024]{1,0:T(8,128)(2,1)S(1)}, u32[]{:S(2)}, u32[]{:S(2)}) collective-permute-start(bf16[512,1024]{1,0:T(8,128)(2,1)} %get-tuple-element.15.refs_0_.refs_4_), channel_id=1, source_target_pairs={{0,8},{1,9},{2,10},{3,11},{4,12},{5,13},{6,14},{7,15},{8,0},{9,1},... | collective-permute-start | bytes 3145736 | tf_op jit(solution)/shard_map/ppermute | solution.py:57
  10.2 47.0 %collective-permute-start = (bf16[512,1024]{1,0:T(8,128)(2,1)}, bf16[512,1024]{1,0:T(8,128)(2,1)S(1)}, u32[]{:S(2)}, u32[]{:S(2)}) collective-permute-start(bf16[512,1024]{1,0:T(8,128)(2,1)} %get-tuple-element.15.refs_0_.refs_4_), channel_id=1, source_target_pairs={{0,2},{1,3},{2,4},{3,5},{4,6},{5,7},{6,0},{7,1},{8,14},{9,15},{10,... | collective-permute-start | bytes 3145736 | tf_op jit(solution)/shard_map/ppermute | solution.py:57
  12.1 46.7 %collective-permute-start.22 = (bf16[512,1024]{1,0:T(8,128)(2,1)}, bf16[512,1024]{1,0:T(8,128)(2,1)S(1)}, u32[]{:S(2)}, u32[]{:S(2)}) collective-permute-start(bf16[512,1024]{1,0:T(8,128)(2,1)} %get-tuple-element.15.refs_0_.refs_4_), channel_id=1, source_target_pairs={{0,64},{1,65},{2,66},{3,67},{4,68},{5,69},{6,70},{7,71},{8,72},{9,... | collective-permute-start | bytes 3145736 | tf_op jit(solution)/shard_map/ppermute | solution.py:57
  21.3 32.4 %collective-permute-start.12 = (bf16[256,1024]{1,0:T(8,128)(2,1)}, bf16[256,1024]{1,0:T(8,128)(2,1)S(1)}, u32[]{:S(2)}, u32[]{:S(2)}) collective-permute-start(bf16[256,1024]{1,0:T(8,128)(2,1)} %get-tuple-element.20), channel_id=1, source_target_pairs={{0,1},{1,0},{2,3},{3,2},{4,5},{5,4},{6,7},{7,6},{8,9},{9,8},{10,11... | collective-permute-start | bytes 1572872 | tf_op jit(solution)/shard_map/ppermute | solution.py:57
  57.3 27.0 %collective-permute-start.9 = (bf16[512,1024]{1,0:T(8,128)(2,1)S(1)}, bf16[512,1024]{1,0:T(8,128)(2,1)}, u32[]{:S(2)}, u32[]{:S(2)}) collective-permute-start(bf16[512,1024]{1,0:T(8,128)(2,1)S(1)} %collective-permute-done.5.refs_6_), channel_id=1, source_target_pairs={{0,16},{1,17},{2,18},{3,19},{4,20},{5,21},{6,22},{7,23},{8,56},{9,... | collective-permute-start | bytes 3145736 | tf_op jit(solution)/shard_map/ppermute | solution.py:57
  58.9 26.4 %collective-permute-start.6 = (bf16[512,1024]{1,0:T(8,128)(2,1)S(1)}, bf16[512,1024]{1,0:T(8,128)(2,1)}, u32[]{:S(2)}, u32[]{:S(2)}) collective-permute-start(bf16[512,1024]{1,0:T(8,128)(2,1)S(1)} %collective-permute-done.1.refs_5_), channel_id=1, source_target_pairs={{0,16},{1,17},{2,18},{3,19},{4,20},{5,21},{6,22},{7,23},{8,56},{9,... | collective-permute-start | bytes 3145736 | tf_op jit(solution)/shard_map/ppermute | solution.py:57
  66.5 16.1 %collective-permute-start.19 = (bf16[256,1024]{1,0:T(8,128)(2,1)S(1)}, bf16[256,1024]{1,0:T(8,128)(2,1)}, u32[]{:S(2)}, u32[]{:S(2)}) collective-permute-start(bf16[256,1024]{1,0:T(8,128)(2,1)S(1)} %collective-permute-done.18), channel_id=1, source_target_pairs={{0,2},{1,3},{2,4},{3,5},{4,6},{5,7},{6,0},{7,1},{8,14},{9,15},{10,... | collective-permute-start | bytes 1572872 | tf_op jit(solution)/shard_map/ppermute | solution.py:57
  72.2 21.8 %collective-permute-start.2 = (bf16[512,1024]{1,0:T(8,128)(2,1)S(1)}, bf16[512,1024]{1,0:T(8,128)(2,1)}, u32[]{:S(2)}, u32[]{:S(2)}) collective-permute-start(bf16[512,1024]{1,0:T(8,128)(2,1)S(1)} %collective-permute-done.1.refs_5_), channel_id=1, source_target_pairs={{0,2},{1,3},{2,4},{3,5},{4,6},{5,7},{6,0},{7,1},{8,14},{9,15},{10,... | collective-permute-start | bytes 3145736 | tf_op jit(solution)/shard_map/ppermute | solution.py:57
  77.0 28.1 %collective-permute-start.4 = (bf16[512,1024]{1,0:T(8,128)(2,1)S(1)}, bf16[512,1024]{1,0:T(8,128)(2,1)S(1)}, u32[]{:S(2)}, u32[]{:S(2)}) collective-permute-start(bf16[512,1024]{1,0:T(8,128)(2,1)S(1)} %collective-permute-done.refs_1_), channel_id=1, source_target_pairs={{0,2},{1,3},{2,4},{3,5},{4,6},{5,7},{6,0},{7,1},{8,14},{9,15},{10,... | collective-permute-start | bytes 3145736 | tf_op jit(solution)/shard_map/ppermute | solution.py:57
  82.7 22.4 %collective-permute-start.24 = (bf16[512,1024]{1,0:T(8,128)(2,1)S(1)}, bf16[512,1024]{1,0:T(8,128)(2,1)}, u32[]{:S(2)}, u32[]{:S(2)}) collective-permute-start(bf16[512,1024]{1,0:T(8,128)(2,1)S(1)} %collective-permute-done.22.refs_7_), channel_id=1, source_target_pairs={{0,16},{1,17},{2,18},{3,19},{4,20},{5,21},{6,22},{7,23},{8,56},{9,... | collective-permute-start | bytes 3145736 | tf_op jit(solution)/shard_map/ppermute | solution.py:57
  84.3 22.4 %collective-permute-start.23 = (bf16[512,1024]{1,0:T(8,128)(2,1)S(1)}, bf16[512,1024]{1,0:T(8,128)(2,1)}, u32[]{:S(2)}, u32[]{:S(2)}) collective-permute-start(bf16[512,1024]{1,0:T(8,128)(2,1)S(1)} %collective-permute-done.22.refs_7_), channel_id=1, source_target_pairs={{0,8},{1,9},{2,10},{3,11},{4,12},{5,13},{6,14},{7,15},{8,0},{9,1},... | collective-permute-start | bytes 3145736 | tf_op jit(solution)/shard_map/ppermute | solution.py:57
  85.3 23.0 %collective-permute-start.8 = (bf16[512,1024]{1,0:T(8,128)(2,1)S(1)}, bf16[512,1024]{1,0:T(8,128)(2,1)S(1)}, u32[]{:S(2)}, u32[]{:S(2)}) collective-permute-start(bf16[512,1024]{1,0:T(8,128)(2,1)S(1)} %collective-permute-done.5.refs_6_), channel_id=1, source_target_pairs={{0,8},{1,9},{2,10},{3,11},{4,12},{5,13},{6,14},{7,15},{8,0},{9,1},... | collective-permute-start | bytes 3145736 | tf_op jit(solution)/shard_map/ppermute | solution.py:57
  93.9 25.3 %collective-permute-start.10 = (bf16[512,1024]{1,0:T(8,128)(2,1)}, bf16[512,1024]{1,0:T(8,128)(2,1)}, u32[]{:S(2)}, u32[]{:S(2)}) collective-permute-start(bf16[512,1024]{1,0:T(8,128)(2,1)} %collective-permute-done.9.refs_10_), channel_id=1, source_target_pairs={{0,8},{1,9},{2,10},{3,11},{4,12},{5,13},{6,14},{7,15},{8,0},{9,1},... | collective-permute-start | bytes 3145736 | tf_op jit(solution)/shard_map/ppermute | solution.py:57
  105.1 16.4 %collective-permute-start.28 = (bf16[512,1024]{1,0:T(8,128)(2,1)}, bf16[512,1024]{1,0:T(8,128)(2,1)}, u32[]{:S(2)}, u32[]{:S(2)}) collective-permute-start(bf16[512,1024]{1,0:T(8,128)(2,1)} %collective-permute-done.24.refs_9_), channel_id=1, source_target_pairs={{0,16},{1,17},{2,18},{3,19},{4,20},{5,21},{6,22},{7,23},{8,56},{9,... | collective-permute-start | bytes 3145736 | tf_op jit(solution)/shard_map/ppermute | solution.py:57
  106.7 26.5 %collective-permute-start.25 = (bf16[512,1024]{1,0:T(8,128)(2,1)}, bf16[512,1024]{1,0:T(8,128)(2,1)}, u32[]{:S(2)}, u32[]{:S(2)}) collective-permute-start(bf16[512,1024]{1,0:T(8,128)(2,1)} %collective-permute-done.23.refs_8_), channel_id=1, source_target_pairs={{0,16},{1,17},{2,18},{3,19},{4,20},{5,21},{6,22},{7,23},{8,56},{9,... | collective-permute-start | bytes 3145736 | tf_op jit(solution)/shard_map/ppermute | solution.py:57
  112.1 21.3 %collective-permute-start.3 = (bf16[512,1024]{1,0:T(8,128)(2,1)}, bf16[512,1024]{1,0:T(8,128)(2,1)}, u32[]{:S(2)}, u32[]{:S(2)}) collective-permute-start(bf16[512,1024]{1,0:T(8,128)(2,1)} %collective-permute-done.2), channel_id=1, source_target_pairs={{0,8},{1,9},{2,10},{3,11},{4,12},{5,13},{6,14},{7,15},{8,0},{9,1},... | collective-permute-start | bytes 3145736 | tf_op jit(solution)/shard_map/ppermute | solution.py:57
  113.9 20.5 %all-to-all-start = ((f32[16,8,128]{2,1,0:T(8,128)}), f32[16,8,128]{2,1,0:T(8,128)S(1)}, u32[]{:S(2)}, u32[]{:S(2)}) async-start(f32[16,8,128]{2,1,0:T(8,128)} %broadcast_in_dim.67), calls=%async_computation | async-start | bytes 131072 | tf_op jit(solution)/shard_map/all_to_all | solution.py:269
  119.3 37.5 %collective-permute-start.27 = (bf16[512,1024]{1,0:T(8,128)(2,1)}, bf16[512,1024]{1,0:T(8,128)(2,1)}, u32[]{:S(2)}, u32[]{:S(2)}) collective-permute-start(bf16[512,1024]{1,0:T(8,128)(2,1)} %collective-permute-done.24.refs_9_), channel_id=1, source_target_pairs={{0,8},{1,9},{2,10},{3,11},{4,12},{5,13},{6,14},{7,15},{8,0},{9,1},... | collective-permute-start | bytes 3145736 | tf_op jit(solution)/shard_map/ppermute | solution.py:57
  119.7 37.0 %collective-permute-start.21 = (bf16[512,1024]{1,0:T(8,128)(2,1)}, bf16[512,1024]{1,0:T(8,128)(2,1)}, u32[]{:S(2)}, u32[]{:S(2)}) collective-permute-start(bf16[512,1024]{1,0:T(8,128)(2,1)} %copy-done.1), channel_id=1, source_target_pairs={{0,1},{1,0},{2,3},{3,2},{4,5},{5,4},{6,7},{7,6},{8,9},{9,8},{10,11... | collective-permute-start | bytes 3145736 | tf_op jit(solution)/shard_map/ppermute | solution.py:57
  121.5 35.3 %collective-permute-start.29 = (bf16[512,1024]{1,0:T(8,128)(2,1)}, bf16[512,1024]{1,0:T(8,128)(2,1)}, u32[]{:S(2)}, u32[]{:S(2)}) collective-permute-start(bf16[512,1024]{1,0:T(8,128)(2,1)} %collective-permute-done.28.refs_13_), channel_id=1, source_target_pairs={{0,8},{1,9},{2,10},{3,11},{4,12},{5,13},{6,14},{7,15},{8,0},{9,1},... | collective-permute-start | bytes 3145736 | tf_op jit(solution)/shard_map/ppermute | solution.py:57
  133.2 23.6 %collective-permute-start.26 = (bf16[512,1024]{1,0:T(8,128)(2,1)}, bf16[512,1024]{1,0:T(8,128)(2,1)}, u32[]{:S(2)}, u32[]{:S(2)}) collective-permute-start(bf16[512,1024]{1,0:T(8,128)(2,1)} %collective-permute-done.25.refs_10_), channel_id=1, source_target_pairs={{0,8},{1,9},{2,10},{3,11},{4,12},{5,13},{6,14},{7,15},{8,0},{9,1},... | collective-permute-start | bytes 3145736 | tf_op jit(solution)/shard_map/ppermute | solution.py:57
  133.4 23.4 %collective-permute-start.20 = (bf16[256,1024]{1,0:T(8,128)(2,1)}, bf16[256,1024]{1,0:T(8,128)(2,1)}, u32[]{:S(2)}, u32[]{:S(2)}) collective-permute-start(bf16[256,1024]{1,0:T(8,128)(2,1)} %collective-permute-done.19), channel_id=1, source_target_pairs={{0,8},{1,9},{2,10},{3,11},{4,12},{5,13},{6,14},{7,15},{8,0},{9,1},... | collective-permute-start | bytes 1572872 | tf_op jit(solution)/shard_map/ppermute | solution.py:57
  176.9 29.1 %all-to-all-start.2 = ((f16[16,512,128]{2,1,0:T(8,128)(2,1)}), f16[16,512,128]{2,1,0:T(8,128)(2,1)S(1)}, u32[]{:S(2)}, u32[]{:S(2)}) async-start(f16[16,512,128]{2,1,0:T(8,128)(2,1)} %gather_fusion), calls=%async_computation.2 | async-start | bytes 4194304 | tf_op jit(solution)/shard_map/all_to_all | solution.py:326
  (32 other events, 299.1 us)

commit v2 on v1

--- a/solution.py
+++ b/solution.py
@@ -12,8 +12,9 @@
 NC = 8
 NR = 16
 CAP = 2
-EARLY_LIMIT = 4 << 20
-LATE_LIMIT = 19 << 20
+EARLY_LIMIT = 8 << 20
+LAST_LIMIT = 4 << 20
+LATE_LIMIT = 32 << 20
 AXES = ("row", "col")
 
 
@@ -57,70 +58,80 @@
     return lax.ppermute(x, AXES, pairs)
 
 
-def mask_kernel(keep_ref, v_ref, m_ref, ma_ref, mb_ref, p_ref):
+def mask_kernel(dev, pattern_ref, v_ref, m_ref, every_ref, p_ref):
     i = pl.program_id(0)
+    nb = ROWS // BLK
 
     @pl.when(i == 0)
     def _():
         p_ref[...] = jnp.zeros_like(p_ref)
 
-    for j in range(COLS // BLK):
+    for j in range(NC):
         sl = pl.ds(j * BLK, BLK)
-        v = v_ref[:, sl]
-        v = jnp.where(keep_ref[i, j] != 0, v, jnp.zeros_like(v))
-        m = v.astype(jnp.bfloat16)
-        m_ref[:, sl] = m
-
-        @pl.when(i < 2)
-        def _():
-            ma_ref[:, sl] = m
-
-        @pl.when(i >= 2)
-        def _():
-            mb_ref[:, sl] = m
-
-        p_ref[:, sl] += jnp.sum(v.reshape(BLK // 8, 8, BLK), axis=0)
-
-
-def mask_and_sum(values, keep):
+        for q in range(nb // 2):
+            rows = pl.ds(q * BLK, BLK)
+            present = pattern_ref[(dev[0] >> 3) * nb + i * (nb // 2) + q, (dev[0] & 7) * NC + j]
+            v = v_ref[rows, sl]
+            v = jnp.where(present != 0, v, jnp.zeros_like(v))
+            m_ref[rows, sl] = v.astype(jnp.bfloat16)
+            p_ref[:, sl] += jnp.sum(v.reshape(BLK // 8, 8, BLK), axis=0)
+
+    @pl.when(i == 1)
+    def _():
+        for j in range(NC):
+            total = jnp.sum(p_ref[:, pl.ds(j * BLK, BLK)], axis=0, keepdims=True)
+            for k in range(NR):
+                every_ref[k, pl.ds(j, 1), :] = total
+
+
+def mask_and_sum(dev, pattern, values):
     return pl.pallas_call(
         mask_kernel,
         grid_spec=pltpu.PrefetchScalarGridSpec(
-            num_scalar_prefetch=1,
-            grid=(ROWS // BLK,),
-            in_specs=[pl.BlockSpec((BLK, COLS), lambda i, k: (i, 0))],
+            num_scalar_prefetch=2,
+            grid=(2,),
+            in_specs=[pl.BlockSpec((ROWS // 2, COLS), lambda i, *_: (i, 0))],
             out_specs=[
-                pl.BlockSpec((BLK, COLS), lambda i, k: (i, 0)),
-                pl.BlockSpec((BLK, COLS), lambda i, k: (jnp.minimum(i, 1), 0)),
-                pl.BlockSpec((BLK, COLS), lambda i, k: (jnp.maximum(i, 2) - 2, 0)),
-                pl.BlockSpec((8, COLS), lambda i, k: (0, 0)),
+                pl.BlockSpec((ROWS // 2, COLS), lambda i, *_: (i, 0)),
+                pl.BlockSpec((NR, NC, BLK), lambda i, *_: (0, 0, 0)),
             ],
+            scratch_shapes=[pltpu.VMEM((8, COLS), jnp.float32)],
         ),
         out_shape=[
             jax.ShapeDtypeStruct((ROWS, COLS), jnp.bfloat16),
-            jax.ShapeDtypeStruct((ROWS // 2, COLS), jnp.bfloat16),
-            jax.ShapeDtypeStruct((ROWS // 2, COLS), jnp.bfloat16),
-            jax.ShapeDtypeStruct((8, COLS), jnp.float32),
-        ],
-    )(keep, values)
+            jax.ShapeDtypeStruct((NR, NC, BLK), jnp.float32),
+        ],
+    )(dev, pattern, values)
 
 
 def early_kernel(meta, keep, outgoing, incoming, inv_ref, *refs):
     del keep, outgoing, incoming
-    a_refs, b_refs = refs[:4], refs[4:12]
-    a_buf, b_buf, acc, sem = refs[12:]
+    a_refs, b_refs, across = refs[:4], refs[4:12], refs[12:16]
+    a_buf, b_buf, acc, third, sem = refs[16:]
     xh, y, t, z, xl = (meta[i] for i in range(5))
     copies = panel_copies(t, z, y, [[r] for r in a_refs], b_refs, a_buf, b_buf, sem)
     for copy in copies[0] + copies[1]:
         copy.start()
+    lo, hi = pl.multiple_of(t * ROWS, ROWS), pl.multiple_of((1 - t) * ROWS, ROWS)
+    even = ((y ^ xl) & 1) == 0
+    for pred, pair in ((even, across[:2]), (jnp.logical_not(even), across[2:])):
+
+        @pl.when(pred)
+        def _(pair=pair):
+            pltpu.make_async_copy(pair[0], third.at[0, pl.ds(lo, ROWS)], sem.at[16]).start()
+            pltpu.make_async_copy(pair[1], third.at[0, pl.ds(hi, ROWS)], sem.at[17]).start()
+
     for copy in copies[0] + copies[1]:
         copy.wait()
-    for k in range(2):
-        part = block_product(inv_ref, a_buf, b_buf, xh, xl + 2 * k)
-        if k == 0:
-            acc[...] = part
-        else:
-            acc[...] += part
+    acc[...] = block_product(inv_ref, a_buf, b_buf, xh, xl)
+    acc[...] += block_product(inv_ref, a_buf, b_buf, xh, xl + 2)
+    pltpu.make_async_copy(across[0], third.at[0, pl.ds(lo, ROWS)], sem.at[16]).wait()
+    pltpu.make_async_copy(across[1], third.at[0, pl.ds(hi, ROWS)], sem.at[17]).wait()
+    acc[...] += block_product(inv_ref, a_buf, third, 1 - xh, third_place(t, y, xl), 0)
+
+
+def third_place(t, y, xl):
+    return jnp.where(((y ^ xl) & 1) == 0, y, (y + 2 * t - 1) & 3)
 
 
 def panel_copies(t, z, y, a_pieces, b_pieces, a_buf, b_buf, sem):
@@ -142,35 +153,39 @@
     return first, second
 
 
-def block_product(inv_ref, a_buf, b_buf, xh, y):
+def block_product(inv_ref, a_buf, b_buf, xh, y, slot=None):
+    slot = y if slot is None else slot
     scale = inv_ref[pl.ds(xh * 4 + y, 1), :]
     a = (a_buf[xh * 2 + (y >> 1)].astype(jnp.float32) * scale).astype(jnp.bfloat16)
-    return jnp.dot(a, b_buf[y], preferred_element_type=jnp.float32)
-
-
-def early_product(meta, tables, inv, a_pieces, b_pieces):
+    return jnp.dot(a, b_buf[slot], preferred_element_type=jnp.float32)
+
+
+def early_product(meta, tables, inv, a_pieces, b_pieces, across):
     anywhere = pl.BlockSpec(memory_space=pltpu.HBM)
     smem = pl.BlockSpec(memory_space=pltpu.SMEM)
     vmem = pl.BlockSpec(memory_space=pltpu.VMEM)
     out = pl.pallas_call(
         early_kernel,
-        in_specs=[smem] * 4 + [vmem] + [anywhere] * 12,
+        in_specs=[smem] * 4 + [vmem] + [anywhere] * 16,
         out_specs=[vmem] * 3,
         out_shape=[
             jax.ShapeDtypeStruct((4, ROWS, COLS), jnp.bfloat16),
             jax.ShapeDtypeStruct((4, 2 * ROWS, COLS), jnp.bfloat16),
             jax.ShapeDtypeStruct((ROWS, COLS), jnp.float32),
         ],
-        scratch_shapes=[pltpu.SemaphoreType.DMA((16,))],
+        scratch_shapes=[
+            pltpu.VMEM((1, 2 * ROWS, COLS), jnp.bfloat16),
+            pltpu.SemaphoreType.DMA((18,)),
+        ],
         compiler_params=pltpu.CompilerParams(vmem_limit_bytes=EARLY_LIMIT),
-    )(meta, *tables, inv, *a_pieces, *b_pieces)
+    )(meta, *tables, inv, *a_pieces, *b_pieces, *across)
     return [pltpu.with_memory_space_constraint(x, pltpu.VMEM) for x in out]
 
 
-def late_kernel(meta, keep, inv_ref, ae_ref, be_ref, part_ref, *refs):
+def late_kernel(meta, keep, outgoing, inv_ref, ae_ref, be_ref, part_ref, *refs):
     a_refs, b_refs = refs[:7], refs[7:15]
-    h_ref, p_ref = refs[15:17]
-    a_buf, b_buf, acc, sem = refs[17:]
+    h_ref, slot_ref = refs[15:17]
+    a_buf, b_buf, acc, p_ref, sem = refs[17:]
     xh, y, t, z, xl = (meta[i] for i in range(5))
     pieces = [a_refs[0:2], a_refs[2:4], a_refs[4:6], a_refs[6:7]]
     first, second = panel_copies(t, z, y, pieces, b_refs, a_buf, b_buf, sem)
@@ -183,8 +198,8 @@
         acc[...] += block_product(inv_ref, a_buf, be_ref, xh, (1 - xl) + 2 * k)
     for copy in second:
         copy.wait()
-    for k in range(2):
-        acc[...] += block_product(inv_ref, ae_ref, b_buf, 1 - xh, xl + 2 * k)
+    rest = (third_place(t, y, xl) + 2) & 3
+    acc[...] += block_product(inv_ref, ae_ref, b_buf, 1 - xh, rest)
     for k in range(2):
         acc[...] += block_product(inv_ref, a_buf, b_buf, 1 - xh, (1 - xl) + 2 * k)
     scale = inv_ref[pl.ds(z * 2 + xl, 1), :]
@@ -201,28 +216,31 @@
         p_ref[pl.ds(j, 1), :] = total
         r = jnp.where(total > 0, 1.0 / total, jnp.zeros_like(total))
         h_ref[j] = h_ref[j] * r * jnp.float32(ROWS)
-
-
-def late_product(meta, keep, inv, early, a_pieces, b_pieces):
+    for k in range(NC * CAP):
+        slot_ref[pl.ds(k, 1), :] = p_ref[pl.ds(outgoing[k], 1), :]
+
+
+def late_product(meta, keep, outgoing, inv, early, a_pieces, b_pieces):
     anywhere = pl.BlockSpec(memory_space=pltpu.HBM)
     smem = pl.BlockSpec(memory_space=pltpu.SMEM)
     vmem = pl.BlockSpec(memory_space=pltpu.VMEM)
     return pl.pallas_call(
         late_kernel,
-        in_specs=[smem, smem] + [vmem] * 4 + [anywhere] * 15,
+        in_specs=[smem] * 3 + [vmem] * 4 + [anywhere] * 15,
         out_specs=[vmem] * 2,
         out_shape=[
             jax.ShapeDtypeStruct((NC, ROWS, BLK), jnp.float32),
-            jax.ShapeDtypeStruct((NC, BLK), jnp.float32),
+            jax.ShapeDtypeStruct((NC * CAP, BLK), jnp.float32),
         ],
         scratch_shapes=[
             pltpu.VMEM((4, ROWS, COLS), jnp.bfloat16),
             pltpu.VMEM((4, 2 * ROWS, COLS), jnp.bfloat16),
             pltpu.VMEM((ROWS, COLS), jnp.float32),
+            pltpu.VMEM((NC, BLK), jnp.float32),
             pltpu.SemaphoreType.DMA((16,)),
         ],
         compiler_params=pltpu.CompilerParams(vmem_limit_bytes=LATE_LIMIT),
-    )(meta, keep, inv, *early, *a_pieces, *b_pieces)
+    )(meta, keep, outgoing, inv, *early, *a_pieces, *b_pieces)
 
 
 def columns_kernel(x_ref, o_ref, sem):
@@ -243,7 +261,7 @@
         out_specs=pl.BlockSpec(memory_space=pltpu.HBM),
         out_shape=jax.ShapeDtypeStruct((ROWS, COLS), jnp.float32),
         scratch_shapes=[pltpu.SemaphoreType.DMA((NC,))],
-        compiler_params=pltpu.CompilerParams(vmem_limit_bytes=EARLY_LIMIT),
+        compiler_params=pltpu.CompilerParams(vmem_limit_bytes=LAST_LIMIT),
     )(pltpu.with_memory_space_constraint(blocks, pltpu.VMEM))
 
 
@@ -265,62 +283,57 @@
     return outgoing.astype(jnp.int32), incoming.astype(jnp.int32)
 
 
-def row_sum(v):
-    every = lax.all_to_all(jnp.broadcast_to(v[None], (NR, NC, BLK)), "row", 0, 0, tiled=True)
-    return jnp.sum(every, axis=0)
-
-
 def body(values, pattern, pruning, owners):
     me_row = lax.axis_index("row").astype(jnp.int32)
     me_col = lax.axis_index("col").astype(jnp.int32)
     meta = jnp.stack([me_row >> 3, (me_row >> 1) & 3, me_row & 1, me_col >> 1, me_col & 1])
     nb = ROWS // BLK
-    present = lax.dynamic_slice(pattern, (me_row * nb, me_col * NC), (nb, NC))
-    keep = lax.dynamic_slice(pruning, (me_row * nb, me_col * NC), (nb, NC)).reshape(nb * NC)
-    m, ma, mb, p = mask_and_sum(values, present)
-    p = jnp.sum(p, axis=0).reshape(NC, BLK)
+    m, every = mask_and_sum((me_row * NC + me_col).reshape(1), pattern, values)
 
     core, ring_z, ring_y = flip("t"), spread("z"), spread("y")
 
     def swap(x):
         return send(x, core)
 
+    keep = lax.dynamic_slice(pruning, (me_row * nb, me_col * NC), (nb, NC))
+    keep = keep.reshape(nb * NC)
     outgoing, incoming = slot_tables(owners, me_col)
-    h = send(m, flip("xh"))
     yu = send(m, ring_y)
     mo = send(m, core)
-    d = row_sum(p)
+    h = send(m, flip("xh"))
     zu = send(m, ring_z)
+    d = jnp.sum(lax.all_to_all(every, "row", 0, 0, tiled=True), axis=0)
     yv = send(mo, ring_y)
     zv = send(mo, ring_z)
-    fa = send(ma, flip("xl"))
-    fb = send(mb, flip("xl"))
+    fa = send(m[: ROWS // 2], flip("xl"))
+    fb = send(m[ROWS // 2 :], flip("xl"))
     yuu = send(yu, ring_y)
     zuu = send(zu, ring_z)
-    inv = jnp.broadcast_to((1.0 / d)[None], (NC, NC, BLK))
-    inv = lax.all_to_all(inv, "col", 0, 0, tiled=True).reshape(NC, COLS)
     ho = send(h, core)
     yh = send(h, ring_y)
     yho = send(ho, ring_y)
+    inv = jnp.broadcast_to((1.0 / d)[None], (NC, NC, BLK))
+    inv = lax.all_to_all(inv, "col", 0, 0, tiled=True).reshape(NC, COLS)
     foa = send(fa, core)
     zfa = send(fa, ring_z)
     zfoa = send(foa, ring_z)
+    xzz = send(zuu, flip("xl"))
     fob = send(fb, core)
     zfb = send(fb, ring_z)
     zfob = send(fob, ring_z)
-    xzz = send(zuu, flip("xl"))
     yhh = send(yh, ring_y)
+    szfoa = send(zfoa, core)
     early = early_product(
         meta, (keep, outgoing, incoming), inv,
         [m, zu, swap(zv), zuu],
         [m, mo, yu, yv, swap(yv), swap(yu), yuu, swap(yuu)],
+        [h, ho, yh, yho],
     )
-    shares, p_out = late_product(
-        meta, keep, inv, early,
-        [fa, fb, zfa, zfb, swap(zfoa), swap(zfob), xzz],
+    shares, sums = late_product(
+        meta, keep, outgoing, inv, early,
+        [fa, fb, zfa, zfb, szfoa, swap(zfob), xzz],
         [h, ho, yh, yho, swap(yho), swap(yh), yhh, swap(yhh)],
     )
-    sums = jnp.take(p_out, outgoing, axis=0, mode="clip")
     sums = lax.all_to_all(sums, "col", 0, 0, tiled=True)
     slots = jnp.take(shares.astype(jnp.float16), outgoing, axis=0, mode="clip")
     arrived = lax.all_to_all(slots, "col", 0, 0, tiled=True)

time: 210 us -> 215 us (1.024)
  local copies, waits for them, and re-layouts: 18.7 us -> 21.2 us
    ppermute x34, waiting for transfers between devices: 103 us -> 94 us  [send(): return lax.ppermute(x, AXES, pairs)]
    all_to_all x1, waiting for transfers between devices: 6.72 us -> 13.7 us  [body(): inv = lax.all_to_all(inv, 'col', 0, 0, tiled=True).reshape(NC, COLS)]
    unnamed x37 -> x45, local copies, waits for them, and re-layouts: 9.69 us -> 14 us
    all_to_all x1, waiting for transfers between devices: 0.17 us -> 2.68 us  [body(): d = jnp.sum(lax.all_to_all(every, 'row', 0, 0, tiled=True), axis=0)]
where the time goes in v2:
time: 215 us; the launch traced here: 213 us
  waiting for transfers between devices  112 us (52%)
  starting transfers between devices  55.1 us (26%)
  Pallas kernels  21.9 us (10%)
  local copies, waits for them, and re-layouts  21.2 us (10%)
  other arithmetic  2.54 us (1%)
    ppermute x34, waiting for transfers between devices, send(): return lax.ppermute(x, AXES, pairs)  94 us
    ppermute x34, starting transfers between devices, send(): return lax.ppermute(x, AXES, pairs)  37 us
    unnamed x45, local copies, waits for them, and re-layouts  14 us
    all_to_all x1, waiting for transfers between devices, body(): inv = lax.all_to_all(inv, 'col', 0, 0, tiled=True).reshape(NC, COLS)  13.7 us
    pallas_call x1, Pallas kernels, late_product(): pl.pallas_call(late_kernel, in_specs=[smem] * 3 + [vmem] * 4 + [anywhere]...  9.73 us
    pallas_call x1, Pallas kernels, early_product(): pl.pallas_call(early_kernel, in_specs=[smem] * 4 + [vmem] + [anywhere] *...  6.96 us
    all_to_all x1, starting transfers between devices, body(): d = jnp.sum(lax.all_to_all(every, 'row', 0, 0, tiled=True), axis=0)  6.74 us
  transfers between devices with their start and end apart: 38, of which 18 were waited for; matrix products, arithmetic and copies ran while one was open for 3% of the time, Pallas kernels for 3%

profile of v2, /device:TPU:0, one launch (start us, length us, event | category | flops | bytes accessed | tf_op | source)
XLA Modules:
  0.0 213.4 jit_solution(67806369428855267)
XLA Ops:
  0.0 3.9 %shard_map.46 = (bf16[512,1024]{1,0:T(8,128)(2,1)}, f32[16,8,128]{2,1,0:T(8,128)}) custom-call(s32[1]{0:T(128)} %bitcast.6.dev, s32[64,64]{1,0:T(8,128)} %pattern_ref.1, f32[512,1024]{1,0:T(8,128)} %v_ref.1), custom_call_target="tpu_custom_call" | custom-call | tf_op jit(solution)/shard_map/pallas_call | solution.py:88
  6.9 2.7 %collective-permute-start.11 = (bf16[512,1024]{1,0:T(8,128)(2,1)S(1)}, bf16[512,1024]{1,0:T(8,128)(2,1)S(1)}, u32[]{:S(2)}, u32[]{:S(2)}) collective-permute-start(bf16[512,1024]{1,0:T(8,128)(2,1)S(1)} %copy-done), channel_id=1, source_target_pairs={{0,64},{1,65},{2,66},{3,67},{4,68},{5,69},{6,70},{7,71},{8,72},{9,... | collective-permute-start | bytes 3145736 | tf_op jit(solution)/shard_map/ppermute | solution.py:58
  13.6 6.5 %collective-permute-done.15.refs_0_ = bf16[256,1024]{1,0:T(8,128)(2,1)S(1)} collective-permute-done((bf16[256,1024]{1,0:T(8,128)(2,1)S(1)}, bf16[256,1024]{1,0:T(8,128)(2,1)S(1)}, u32[]{:S(2)}, u32[]{:S(2)}) %collective-permute-start.15) | collective-permute-done | bytes 524320 | tf_op jit(solution)/shard_map/ppermute | solution.py:58
  21.7 30.8 %collective-permute-done.16.refs_1_ = bf16[256,1024]{1,0:T(8,128)(2,1)S(1)} collective-permute-done((bf16[256,1024]{1,0:T(8,128)(2,1)S(1)}, bf16[256,1024]{1,0:T(8,128)(2,1)S(1)}, u32[]{:S(2)}, u32[]{:S(2)}) %collective-permute-start.16) | collective-permute-done | bytes 524320 | tf_op jit(solution)/shard_map/ppermute | solution.py:58
  53.1 2.2 %collective-permute-start.17 = (bf16[256,1024]{1,0:T(8,128)(2,1)S(1)}, bf16[256,1024]{1,0:T(8,128)(2,1)S(1)}, u32[]{:S(2)}, u32[]{:S(2)}) collective-permute-start(bf16[256,1024]{1,0:T(8,128)(2,1)S(1)} %collective-permute-done.15.refs_0_), channel_id=1, source_target_pairs={{0,2},{1,3},{2,4},{3,5},{4,6},{5,7},{6,0},{7,1},{8,14},{9,15},{10,... | collective-permute-start | bytes 1572872 | tf_op jit(solution)/shard_map/ppermute | solution.py:58
  62.0 2.5 %collective-permute-done.17.refs_2_ = bf16[256,1024]{1,0:T(8,128)(2,1)S(1)} collective-permute-done((bf16[256,1024]{1,0:T(8,128)(2,1)S(1)}, bf16[256,1024]{1,0:T(8,128)(2,1)S(1)}, u32[]{:S(2)}, u32[]{:S(2)}) %collective-permute-start.17) | collective-permute-done | bytes 524320 | tf_op jit(solution)/shard_map/ppermute | solution.py:58
  65.3 4.8 %collective-permute-done.18.refs_3_ = bf16[256,1024]{1,0:T(8,128)(2,1)S(1)} collective-permute-done((bf16[256,1024]{1,0:T(8,128)(2,1)S(1)}, bf16[256,1024]{1,0:T(8,128)(2,1)S(1)}, u32[]{:S(2)}, u32[]{:S(2)}) %collective-permute-start.18) | collective-permute-done | bytes 524320 | tf_op jit(solution)/shard_map/ppermute | solution.py:58
  72.5 3.2 %collective-permute-done.20 = bf16[256,1024]{1,0:T(8,128)(2,1)S(1)} collective-permute-done((bf16[256,1024]{1,0:T(8,128)(2,1)S(1)}, bf16[256,1024]{1,0:T(8,128)(2,1)S(1)}, u32[]{:S(2)}, u32[]{:S(2)}) %collective-permute-start.20) | collective-permute-done | bytes 524320 | tf_op jit(solution)/shard_map/ppermute | solution.py:58
  77.3 4.1 %collective-permute-done.23 = bf16[256,1024]{1,0:T(8,128)(2,1)} collective-permute-done((bf16[256,1024]{1,0:T(8,128)(2,1)S(1)}, bf16[256,1024]{1,0:T(8,128)(2,1)}, u32[]{:S(2)}, u32[]{:S(2)}) %collective-permute-start.23) | collective-permute-done | bytes 524320 | tf_op jit(solution)/shard_map/ppermute | solution.py:58
  87.8 10.4 %collective-permute-done.6.refs_7_ = bf16[512,1024]{1,0:T(8,128)(2,1)} collective-permute-done((bf16[512,1024]{1,0:T(8,128)(2,1)S(1)}, bf16[512,1024]{1,0:T(8,128)(2,1)}, u32[]{:S(2)}, u32[]{:S(2)}) %collective-permute-start.6) | collective-permute-done | bytes 1048608 | tf_op jit(solution)/shard_map/ppermute | solution.py:58
  98.8 9.9 %collective-permute-done.4.refs_3_ = bf16[512,1024]{1,0:T(8,128)(2,1)S(1)} collective-permute-done((bf16[512,1024]{1,0:T(8,128)(2,1)S(1)}, bf16[512,1024]{1,0:T(8,128)(2,1)S(1)}, u32[]{:S(2)}, u32[]{:S(2)}) %collective-permute-start.4) | collective-permute-done | bytes 1048608 | tf_op jit(solution)/shard_map/ppermute | solution.py:58
  114.1 6.7 %all-to-all-start = ((f32[16,8,128]{2,1,0:T(8,128)}), f32[16,8,128]{2,1,0:T(8,128)S(1)}, u32[]{:S(2)}, u32[]{:S(2)}) async-start(f32[16,8,128]{2,1,0:T(8,128)} %get-tuple-element.12), calls=%async_computation | async-start | bytes 131072 | tf_op jit(solution)/shard_map/all_to_all | solution.py:305
  122.1 3.0 %collective-permute-done.28.refs_13_ = bf16[512,1024]{1,0:T(8,128)(2,1)} collective-permute-done((bf16[512,1024]{1,0:T(8,128)(2,1)}, bf16[512,1024]{1,0:T(8,128)(2,1)}, u32[]{:S(2)}, u32[]{:S(2)}) %collective-permute-start.28) | collective-permute-done | bytes 1048608 | tf_op jit(solution)/shard_map/ppermute | solution.py:58
  125.9 2.7 %all-to-all-done = f32[16,8,128]{2,1,0:T(8,128)S(1)} async-done(((f32[16,8,128]{2,1,0:T(8,128)}), f32[16,8,128]{2,1,0:T(8,128)S(1)}, u32[]{:S(2)}, u32[]{:S(2)}) %all-to-all-start) | async-done | bytes 65568 | tf_op jit(solution)/shard_map/all_to_all | solution.py:305
  129.2 3.3 %all-to-all-start.1 = ((f32[8,8,128]{2,1,0:T(8,128)}), f32[8,8,128]{2,1,0:T(8,128)S(1)}, u32[]{:S(2)}, u32[]{:S(2)}) async-start(f32[8,8,128]{2,1,0:T(8,128)} %broadcast_in_dim.61), calls=%async_computation.1 | async-start | bytes 65536 | tf_op jit(solution)/shard_map/all_to_all | solution.py:316
  133.8 13.7 %all-to-all-done.1 = f32[8,8,128]{2,1,0:T(8,128)S(1)} async-done(((f32[8,8,128]{2,1,0:T(8,128)}), f32[8,8,128]{2,1,0:T(8,128)S(1)}, u32[]{:S(2)}, u32[]{:S(2)}) %all-to-all-start.1) | async-done | bytes 32800 | tf_op jit(solution)/shard_map/all_to_all | solution.py:316
  153.6 7.0 %shard_map.47 = (bf16[4,512,1024]{2,1,0:T(8,128)(2,1)S(1)}, bf16[4,1024,1024]{2,1,0:T(8,128)(2,1)S(1)}, f32[512,1024]{1,0:T(8,128)S(1)}) custom-call(s32[5]{0:T(128)S(1)} %stack.23.meta, s32[32]{0:T(128)S(1)} %reshape.111.keep, s32[16]{0:T(128)S(1)} %select_reduce_fusion.2.outgoing, s32[8]{0:T(128)S(1)} %select_reduce_fusion.incoming, ...), custom_call_target="tpu_custom_call" | custom-call | tf_op jit(solution)/shard_map/pallas_call | solution.py:167
  160.7 9.7 %shard_map.48 = (f32[8,512,128]{2,1,0:T(8,128)}, f32[16,128]{1,0:T(8,128)}) custom-call(s32[5]{0:T(128)S(1)} %stack.23.meta, s32[32]{0:T(128)S(1)} %reshape.111.keep, s32[16]{0:T(128)S(1)} %select_reduce_fusion.2.outgoing, f32[8,1024]{1,0:T(8,128)S(1)} %bitcast.15, bf16[4,512,1024]{2,1,0:T(8,128)(2,1)S(1)} %get-tuple-element.14.ae_ref, ...), custom_call_target="tpu_custom_call" | custom-call | tf_op jit(solution)/shard_map/pallas_call | solution.py:227
  170.4 4.1 %all-to-all-start.3 = ((f32[8,2,128]{2,1,0:T(2,128)}), f32[8,2,128]{2,1,0:T(2,128)S(1)}, u32[]{:S(2)}, u32[]{:S(2)}) async-start(f32[8,2,128]{2,1,0:T(2,128)} %bitcast.7), calls=%async_computation.3 | async-start | bytes 16384 | tf_op jit(solution)/shard_map/all_to_all | solution.py:337
  176.3 2.7 %gather_fusion = f16[16,512,128]{2,1,0:T(8,128)(2,1)} fusion(f16[8,512,128]{2,1,0:T(8,128)(2,1)S(1)} %convert_element_type.6, s32[1024]{0:T(1024)S(1)} %pad_clamp_fusion.1), kind=kCustom, calls=%fused_computation | custom fusion | bytes 4194368 | tf_op jit(solution)/shard_map/jit(_take)/gather | solution.py:338
  180.7 4.0 %all-to-all-start.2 = ((f16[16,512,128]{2,1,0:T(8,128)(2,1)}), f16[16,512,128]{2,1,0:T(8,128)(2,1)S(1)}, u32[]{:S(2)}, u32[]{:S(2)}) async-start(f16[16,512,128]{2,1,0:T(8,128)(2,1)} %gather_fusion), calls=%async_computation.2 | async-start | bytes 4194304 | tf_op jit(solution)/shard_map/all_to_all | solution.py:339
  190.1 3.4 %collective-permute-start.32 = (f32[8,128]{1,0:T(8,128)S(1)}, f32[8,128]{1,0:T(8,128)S(1)}, u32[]{:S(2)}, u32[]{:S(2)}) collective-permute-start(f32[8,128]{1,0:T(8,128)S(1)} %add.69), channel_id=1, source_target_pairs={{0,32},{1,33},{2,34},{3,35},{4,36},{5,37},{6,38},{7,39},{8,40},{9,... | collective-permute-start | bytes 12296 | tf_op jit(solution)/shard_map/ppermute | solution.py:58
  195.2 4.0 %collective-permute-start.33 = (f32[8,128]{1,0:T(8,128)S(1)}, f32[8,128]{1,0:T(8,128)S(1)}, u32[]{:S(2)}, u32[]{:S(2)}) collective-permute-start(f32[8,128]{1,0:T(8,128)S(1)} %add.70), channel_id=1, source_target_pairs={{0,64},{1,65},{2,66},{3,67},{4,68},{5,69},{6,70},{7,71},{8,72},{9,... | collective-permute-start | bytes 12296 | tf_op jit(solution)/shard_map/ppermute | solution.py:58
  199.2 11.5 %collective-permute-done.33 = f32[8,128]{1,0:T(8,128)S(1)} collective-permute-done((f32[8,128]{1,0:T(8,128)S(1)}, f32[8,128]{1,0:T(8,128)S(1)}, u32[]{:S(2)}, u32[]{:S(2)}) %collective-permute-start.33) | collective-permute-done | bytes 4128 | tf_op jit(solution)/shard_map/ppermute | solution.py:58
  (129 shorter events, 56.1 us)
Async XLA Ops:
  6.9 45.6 %collective-permute-start.11 = (bf16[512,1024]{1,0:T(8,128)(2,1)S(1)}, bf16[512,1024]{1,0:T(8,128)(2,1)S(1)}, u32[]{:S(2)}, u32[]{:S(2)}) collective-permute-start(bf16[512,1024]{1,0:T(8,128)(2,1)S(1)} %copy-done), channel_id=1, source_target_pairs={{0,64},{1,65},{2,66},{3,67},{4,68},{5,69},{6,70},{7,71},{8,72},{9,... | collective-permute-start | bytes 3145736 | tf_op jit(solution)/shard_map/ppermute | solution.py:58
  9.7 43.4 %collective-permute-start.5 = (bf16[512,1024]{1,0:T(8,128)(2,1)S(1)}, bf16[512,1024]{1,0:T(8,128)(2,1)S(1)}, u32[]{:S(2)}, u32[]{:S(2)}) collective-permute-start(bf16[512,1024]{1,0:T(8,128)(2,1)S(1)} %copy-done), channel_id=1, source_target_pairs={{0,16},{1,17},{2,18},{3,19},{4,20},{5,21},{6,22},{7,23},{8,56},{9,... | collective-permute-start | bytes 3145736 | tf_op jit(solution)/shard_map/ppermute | solution.py:58
  11.2 44.8 %collective-permute-start.1 = (bf16[512,1024]{1,0:T(8,128)(2,1)S(1)}, bf16[512,1024]{1,0:T(8,128)(2,1)S(1)}, u32[]{:S(2)}, u32[]{:S(2)}) collective-permute-start(bf16[512,1024]{1,0:T(8,128)(2,1)S(1)} %copy-done), channel_id=1, source_target_pairs={{0,8},{1,9},{2,10},{3,11},{4,12},{5,13},{6,14},{7,15},{8,0},{9,1},... | collective-permute-start | bytes 3145736 | tf_op jit(solution)/shard_map/ppermute | solution.py:58
  11.7 46.3 %collective-permute-start = (bf16[512,1024]{1,0:T(8,128)(2,1)S(1)}, bf16[512,1024]{1,0:T(8,128)(2,1)S(1)}, u32[]{:S(2)}, u32[]{:S(2)}) collective-permute-start(bf16[512,1024]{1,0:T(8,128)(2,1)S(1)} %copy-done), channel_id=1, source_target_pairs={{0,2},{1,3},{2,4},{3,5},{4,6},{5,7},{6,0},{7,1},{8,14},{9,15},{10,... | collective-permute-start | bytes 3145736 | tf_op jit(solution)/shard_map/ppermute | solution.py:58
  20.1 32.4 %collective-permute-start.16 = (bf16[256,1024]{1,0:T(8,128)(2,1)S(1)}, bf16[256,1024]{1,0:T(8,128)(2,1)S(1)}, u32[]{:S(2)}, u32[]{:S(2)}) collective-permute-start(bf16[256,1024]{1,0:T(8,128)(2,1)S(1)} %get-tuple-element.19), channel_id=1, source_target_pairs={{0,1},{1,0},{2,3},{3,2},{4,5},{5,4},{6,7},{7,6},{8,9},{9,8},{10,11... | collective-permute-start | bytes 1572872 | tf_op jit(solution)/shard_map/ppermute | solution.py:58
  56.0 26.4 %collective-permute-start.12 = (bf16[512,1024]{1,0:T(8,128)(2,1)S(1)}, bf16[512,1024]{1,0:T(8,128)(2,1)S(1)}, u32[]{:S(2)}, u32[]{:S(2)}) collective-permute-start(bf16[512,1024]{1,0:T(8,128)(2,1)S(1)} %collective-permute-done.11.refs_12_.refs_7_), channel_id=1, source_target_pairs={{0,8},{1,9},{2,10},{3,11},{4,12},{5,13},{6,14},{7,15},{8,0},{9,1},... | collective-permute-start | bytes 3145736 | tf_op jit(solution)/shard_map/ppermute | solution.py:58
  57.9 27.3 %collective-permute-start.13 = (bf16[512,1024]{1,0:T(8,128)(2,1)S(1)}, bf16[512,1024]{1,0:T(8,128)(2,1)}, u32[]{:S(2)}, u32[]{:S(2)}) collective-permute-start(bf16[512,1024]{1,0:T(8,128)(2,1)S(1)} %collective-permute-done.11.refs_12_.refs_7_), channel_id=1, source_target_pairs={{0,16},{1,17},{2,18},{3,19},{4,20},{5,21},{6,22},{7,23},{8,56},{9,... | collective-permute-start | bytes 3145736 | tf_op jit(solution)/shard_map/ppermute | solution.py:58
  65.3 16.2 %collective-permute-start.23 = (bf16[256,1024]{1,0:T(8,128)(2,1)S(1)}, bf16[256,1024]{1,0:T(8,128)(2,1)}, u32[]{:S(2)}, u32[]{:S(2)}) collective-permute-start(bf16[256,1024]{1,0:T(8,128)(2,1)S(1)} %collective-permute-done.22), channel_id=1, source_target_pairs={{0,2},{1,3},{2,4},{3,5},{4,6},{5,7},{6,0},{7,1},{8,14},{9,15},{10,... | collective-permute-start | bytes 1572872 | tf_op jit(solution)/shard_map/ppermute | solution.py:58
  70.9 16.1 %collective-permute-start.9 = (bf16[512,1024]{1,0:T(8,128)(2,1)S(1)}, bf16[512,1024]{1,0:T(8,128)(2,1)}, u32[]{:S(2)}, u32[]{:S(2)}) collective-permute-start(bf16[512,1024]{1,0:T(8,128)(2,1)S(1)} %collective-permute-done.5.refs_6_), channel_id=1, source_target_pairs={{0,16},{1,17},{2,18},{3,19},{4,20},{5,21},{6,22},{7,23},{8,56},{9,... | collective-permute-start | bytes 3145736 | tf_op jit(solution)/shard_map/ppermute | solution.py:58
  75.7 22.5 %collective-permute-start.6 = (bf16[512,1024]{1,0:T(8,128)(2,1)S(1)}, bf16[512,1024]{1,0:T(8,128)(2,1)}, u32[]{:S(2)}, u32[]{:S(2)}) collective-permute-start(bf16[512,1024]{1,0:T(8,128)(2,1)S(1)} %collective-permute-done.1.refs_5_), channel_id=1, source_target_pairs={{0,16},{1,17},{2,18},{3,19},{4,20},{5,21},{6,22},{7,23},{8,56},{9,... | collective-permute-start | bytes 3145736 | tf_op jit(solution)/shard_map/ppermute | solution.py:58
  81.5 16.8 %collective-permute-start.2 = (bf16[512,1024]{1,0:T(8,128)(2,1)S(1)}, bf16[512,1024]{1,0:T(8,128)(2,1)}, u32[]{:S(2)}, u32[]{:S(2)}) collective-permute-start(bf16[512,1024]{1,0:T(8,128)(2,1)S(1)} %collective-permute-done.1.refs_5_), channel_id=1, source_target_pairs={{0,2},{1,3},{2,4},{3,5},{4,6},{5,7},{6,0},{7,1},{8,14},{9,15},{10,... | collective-permute-start | bytes 3145736 | tf_op jit(solution)/shard_map/ppermute | solution.py:58
  82.5 26.3 %collective-permute-start.4 = (bf16[512,1024]{1,0:T(8,128)(2,1)S(1)}, bf16[512,1024]{1,0:T(8,128)(2,1)S(1)}, u32[]{:S(2)}, u32[]{:S(2)}) collective-permute-start(bf16[512,1024]{1,0:T(8,128)(2,1)S(1)} %collective-permute-done.refs_1_), channel_id=1, source_target_pairs={{0,2},{1,3},{2,4},{3,5},{4,6},{5,7},{6,0},{7,1},{8,14},{9,15},{10,... | collective-permute-start | bytes 3145736 | tf_op jit(solution)/shard_map/ppermute | solution.py:58
  85.2 25.1 %collective-permute-start.8 = (bf16[512,1024]{1,0:T(8,128)(2,1)S(1)}, bf16[512,1024]{1,0:T(8,128)(2,1)S(1)}, u32[]{:S(2)}, u32[]{:S(2)}) collective-permute-start(bf16[512,1024]{1,0:T(8,128)(2,1)S(1)} %collective-permute-done.5.refs_6_), channel_id=1, source_target_pairs={{0,8},{1,9},{2,10},{3,11},{4,12},{5,13},{6,14},{7,15},{8,0},{9,1},... | collective-permute-start | bytes 3145736 | tf_op jit(solution)/shard_map/ppermute | solution.py:58
  87.0 33.9 %collective-permute-start.14 = (bf16[512,1024]{1,0:T(8,128)(2,1)S(1)}, bf16[512,1024]{1,0:T(8,128)(2,1)}, u32[]{:S(2)}, u32[]{:S(2)}) collective-permute-start(bf16[512,1024]{1,0:T(8,128)(2,1)S(1)} %collective-permute-done.12.refs_13_.refs_8_), channel_id=1, source_target_pairs={{0,16},{1,17},{2,18},{3,19},{4,20},{5,21},{6,22},{7,23},{8,56},{9,... | collective-permute-start | bytes 3145736 | tf_op jit(solution)/shard_map/ppermute | solution.py:58
  98.3 23.2 %collective-permute-start.10 = (bf16[512,1024]{1,0:T(8,128)(2,1)}, bf16[512,1024]{1,0:T(8,128)(2,1)}, u32[]{:S(2)}, u32[]{:S(2)}) collective-permute-start(bf16[512,1024]{1,0:T(8,128)(2,1)} %collective-permute-done.9.refs_10_), channel_id=1, source_target_pairs={{0,8},{1,9},{2,10},{3,11},{4,12},{5,13},{6,14},{7,15},{8,0},{9,1},... | collective-permute-start | bytes 3145736 | tf_op jit(solution)/shard_map/ppermute | solution.py:58
  98.3 23.8 %collective-permute-start.7 = (bf16[512,1024]{1,0:T(8,128)(2,1)}, bf16[512,1024]{1,0:T(8,128)(2,1)}, u32[]{:S(2)}, u32[]{:S(2)}) collective-permute-start(bf16[512,1024]{1,0:T(8,128)(2,1)} %collective-permute-done.6.refs_7_), channel_id=1, source_target_pairs={{0,8},{1,9},{2,10},{3,11},{4,12},{5,13},{6,14},{7,15},{8,0},{9,1},... | collective-permute-start | bytes 3145736 | tf_op jit(solution)/shard_map/ppermute | solution.py:58
  108.7 16.3 %collective-permute-start.28 = (bf16[512,1024]{1,0:T(8,128)(2,1)}, bf16[512,1024]{1,0:T(8,128)(2,1)}, u32[]{:S(2)}, u32[]{:S(2)}) collective-permute-start(bf16[512,1024]{1,0:T(8,128)(2,1)} %collective-permute-done.13.refs_14_.refs_9_), channel_id=1, source_target_pairs={{0,16},{1,17},{2,18},{3,19},{4,20},{5,21},{6,22},{7,23},{8,56},{9,... | collective-permute-start | bytes 3145736 | tf_op jit(solution)/shard_map/ppermute | solution.py:58
  121.0 39.6 %collective-permute-start.27 = (bf16[512,1024]{1,0:T(8,128)(2,1)}, bf16[512,1024]{1,0:T(8,128)(2,1)}, u32[]{:S(2)}, u32[]{:S(2)}) collective-permute-start(bf16[512,1024]{1,0:T(8,128)(2,1)} %collective-permute-done.13.refs_14_.refs_9_), channel_id=1, source_target_pairs={{0,8},{1,9},{2,10},{3,11},{4,12},{5,13},{6,14},{7,15},{8,0},{9,1},... | collective-permute-start | bytes 3145736 | tf_op jit(solution)/shard_map/ppermute | solution.py:58
  121.5 39.1 %collective-permute-start.25 = (bf16[512,1024]{1,0:T(8,128)(2,1)}, bf16[512,1024]{1,0:T(8,128)(2,1)}, u32[]{:S(2)}, u32[]{:S(2)}) collective-permute-start(bf16[512,1024]{1,0:T(8,128)(2,1)} %copy-done.7), channel_id=1, source_target_pairs={{0,1},{1,0},{2,3},{3,2},{4,5},{5,4},{6,7},{7,6},{8,9},{9,8},{10,11... | collective-permute-start | bytes 3145736 | tf_op jit(solution)/shard_map/ppermute | solution.py:58
  122.1 38.5 %collective-permute-start.26 = (bf16[512,1024]{1,0:T(8,128)(2,1)}, bf16[512,1024]{1,0:T(8,128)(2,1)}, u32[]{:S(2)}, u32[]{:S(2)}) collective-permute-start(bf16[512,1024]{1,0:T(8,128)(2,1)} %collective-permute-done.14.refs_15_.refs_10_), channel_id=1, source_target_pairs={{0,8},{1,9},{2,10},{3,11},{4,12},{5,13},{6,14},{7,15},{8,0},{9,1},... | collective-permute-start | bytes 3145736 | tf_op jit(solution)/shard_map/ppermute | solution.py:58
  125.0 35.6 %collective-permute-start.29 = (bf16[512,1024]{1,0:T(8,128)(2,1)}, bf16[512,1024]{1,0:T(8,128)(2,1)}, u32[]{:S(2)}, u32[]{:S(2)}) collective-permute-start(bf16[512,1024]{1,0:T(8,128)(2,1)} %collective-permute-done.28.refs_13_), channel_id=1, source_target_pairs={{0,8},{1,9},{2,10},{3,11},{4,12},{5,13},{6,14},{7,15},{8,0},{9,1},... | collective-permute-start | bytes 3145736 | tf_op jit(solution)/shard_map/ppermute | solution.py:58
  125.2 35.4 %collective-permute-start.24 = (bf16[256,1024]{1,0:T(8,128)(2,1)}, bf16[256,1024]{1,0:T(8,128)(2,1)}, u32[]{:S(2)}, u32[]{:S(2)}) collective-permute-start(bf16[256,1024]{1,0:T(8,128)(2,1)} %collective-permute-done.23), channel_id=1, source_target_pairs={{0,8},{1,9},{2,10},{3,11},{4,12},{5,13},{6,14},{7,15},{8,0},{9,1},... | collective-permute-start | bytes 1572872 | tf_op jit(solution)/shard_map/ppermute | solution.py:58
  129.2 18.3 %all-to-all-start.1 = ((f32[8,8,128]{2,1,0:T(8,128)}), f32[8,8,128]{2,1,0:T(8,128)S(1)}, u32[]{:S(2)}, u32[]{:S(2)}) async-start(f32[8,8,128]{2,1,0:T(8,128)} %broadcast_in_dim.61), calls=%async_computation.1 | async-start | bytes 65536 | tf_op jit(solution)/shard_map/all_to_all | solution.py:316
  180.7 30.0 %all-to-all-start.2 = ((f16[16,512,128]{2,1,0:T(8,128)(2,1)}), f16[16,512,128]{2,1,0:T(8,128)(2,1)S(1)}, u32[]{:S(2)}, u32[]{:S(2)}) async-start(f16[16,512,128]{2,1,0:T(8,128)(2,1)} %gather_fusion), calls=%async_computation.2 | async-start | bytes 4194304 | tf_op jit(solution)/shard_map/all_to_all | solution.py:339
  (36 other events, 305.2 us)

commit v3 on v2

--- a/solution.py
+++ b/solution.py
@@ -14,7 +14,7 @@
 CAP = 2
 EARLY_LIMIT = 8 << 20
 LAST_LIMIT = 4 << 20
-LATE_LIMIT = 32 << 20
+LATE_LIMIT = 19 << 20
 AXES = ("row", "col")
 
 
@@ -182,45 +182,64 @@
     return [pltpu.with_memory_space_constraint(x, pltpu.VMEM) for x in out]
 
 
-def late_kernel(meta, keep, outgoing, inv_ref, ae_ref, be_ref, part_ref, *refs):
+def late_kernel(meta, keep, slots, inv_ref, ae_ref, be_ref, part_ref, *refs):
     a_refs, b_refs = refs[:7], refs[7:15]
     h_ref, slot_ref = refs[15:17]
-    a_buf, b_buf, acc, p_ref, sem = refs[17:]
+    a_buf, b_buf, acc, sem = refs[17:]
     xh, y, t, z, xl = (meta[i] for i in range(5))
     pieces = [a_refs[0:2], a_refs[2:4], a_refs[4:6], a_refs[6:7]]
     first, second = panel_copies(t, z, y, pieces, b_refs, a_buf, b_buf, sem)
-    for copy in first + second:
+    even = ((y ^ xl) & 1) == 0
+    for copy in first:
         copy.start()
+    for n, pred in ((0, jnp.logical_not(even)), (1, even)):
+
+        @pl.when(pred)
+        def _(pair=second[2 * n : 2 * n + 2]):
+            for copy in pair:
+                copy.start()
+
+    for copy in second[4:]:
+        copy.start()
+    for k in range(NC * CAP):
+        h_ref[k] = jnp.zeros((ROWS, BLK), jnp.float32)
     for copy in first:
         copy.wait()
     acc[...] = part_ref[...]
     for k in range(2):
         acc[...] += block_product(inv_ref, a_buf, be_ref, xh, (1 - xl) + 2 * k)
-    for copy in second:
+    for n, pred in ((0, jnp.logical_not(even)), (1, even)):
+
+        @pl.when(pred)
+        def _(pair=second[2 * n : 2 * n + 2]):
+            for copy in pair:
+                copy.wait()
+
+    for copy in second[4:]:
         copy.wait()
     rest = (third_place(t, y, xl) + 2) & 3
     acc[...] += block_product(inv_ref, ae_ref, b_buf, 1 - xh, rest)
     for k in range(2):
         acc[...] += block_product(inv_ref, a_buf, b_buf, 1 - xh, (1 - xl) + 2 * k)
     scale = inv_ref[pl.ds(z * 2 + xl, 1), :]
+    slot_ref[...] = jnp.zeros_like(slot_ref)
     for j in range(NC):
         sl = pl.ds(j * BLK, BLK)
+        slot = slots[j]
         total = jnp.zeros((8, BLK), jnp.float32)
         for i in range(ROWS // BLK):
             rows = pl.ds(i * BLK, BLK)
             g = acc[rows, sl] * scale[:, j * BLK : (j + 1) * BLK]
             g = jnp.where(keep[i * NC + j] != 0, g * g, jnp.zeros_like(g))
-            h_ref[j, rows] = g
+            acc[rows, sl] = g
             total += jnp.sum(g.reshape(BLK // 8, 8, BLK), axis=0)
         total = jnp.sum(total, axis=0, keepdims=True)
-        p_ref[pl.ds(j, 1), :] = total
+        slot_ref[pl.ds(slot, 1), :] = total
         r = jnp.where(total > 0, 1.0 / total, jnp.zeros_like(total))
-        h_ref[j] = h_ref[j] * r * jnp.float32(ROWS)
-    for k in range(NC * CAP):
-        slot_ref[pl.ds(k, 1), :] = p_ref[pl.ds(outgoing[k], 1), :]
-
-
-def late_product(meta, keep, outgoing, inv, early, a_pieces, b_pieces):
+        h_ref[slot] = acc[:, sl] * r * jnp.float32(ROWS)
+
+
+def late_product(meta, keep, slots, inv, early, a_pieces, b_pieces):
     anywhere = pl.BlockSpec(memory_space=pltpu.HBM)
     smem = pl.BlockSpec(memory_space=pltpu.SMEM)
     vmem = pl.BlockSpec(memory_space=pltpu.VMEM)
@@ -229,18 +248,17 @@
         in_specs=[smem] * 3 + [vmem] * 4 + [anywhere] * 15,
         out_specs=[vmem] * 2,
         out_shape=[
-            jax.ShapeDtypeStruct((NC, ROWS, BLK), jnp.float32),
+            jax.ShapeDtypeStruct((NC * CAP, ROWS, BLK), jnp.float32),
             jax.ShapeDtypeStruct((NC * CAP, BLK), jnp.float32),
         ],
         scratch_shapes=[
             pltpu.VMEM((4, ROWS, COLS), jnp.bfloat16),
             pltpu.VMEM((4, 2 * ROWS, COLS), jnp.bfloat16),
             pltpu.VMEM((ROWS, COLS), jnp.float32),
-            pltpu.VMEM((NC, BLK), jnp.float32),
             pltpu.SemaphoreType.DMA((16,)),
         ],
         compiler_params=pltpu.CompilerParams(vmem_limit_bytes=LATE_LIMIT),
-    )(meta, keep, outgoing, inv, *early, *a_pieces, *b_pieces)
+    )(meta, keep, slots, inv, *early, *a_pieces, *b_pieces)
 
 
 def columns_kernel(x_ref, o_ref, sem):
@@ -271,11 +289,9 @@
     earlier = jnp.arange(NC)[:, None] < jnp.arange(NC)[None, :]
     same = dest[:, :, None] == dest[:, None, :]
     rank = jnp.sum(jnp.where(same & earlier, 1, 0), axis=1)
-    slots = jnp.arange(NC * CAP)
     mine = lax.dynamic_slice(dest, (me_col, 0), (1, NC))[0]
     my_rank = lax.dynamic_slice(rank, (me_col, 0), (1, NC))[0]
-    hit = (mine[None, :] * CAP + my_rank[None, :]) == slots[:, None]
-    outgoing = jnp.sum(jnp.where(hit, jnp.arange(NC)[None, :], 0), axis=1)
+    outgoing = mine * CAP + my_rank
     slot_of = jnp.arange(NC)[:, None] * CAP + rank
     wanted = me_col * NC + jnp.arange(NC)
     match = table[None] == wanted[:, None, None]
@@ -334,8 +350,8 @@
         [fa, fb, zfa, zfb, szfoa, swap(zfob), xzz],
         [h, ho, yh, yho, swap(yho), swap(yh), yhh, swap(yhh)],
     )
+    slots, sums = lax.optimization_barrier((shares.astype(jnp.float16), sums))
     sums = lax.all_to_all(sums, "col", 0, 0, tiled=True)
-    slots = jnp.take(shares.astype(jnp.float16), outgoing, axis=0, mode="clip")
     arrived = lax.all_to_all(slots, "col", 0, 0, tiled=True)
     sums = jnp.take(sums, incoming, axis=0, mode="clip")
     total = sums + send(sums, core)

time: 215 us -> 214 us (level)
  blocking collectives: 0 us -> 10 us
  starting transfers between devices: 55.1 us -> 50.7 us
  local copies, waits for them, and re-layouts: 21.2 us -> 18.5 us
    all_to_all x0 -> x1, blocking collectives: none -> 10 us  [body(): sums = lax.all_to_all(sums, 'col', 0, 0, tiled=True)]
    all_to_all x1 -> x0, starting transfers between devices: 4.07 us -> none  [body(): sums = lax.all_to_all(sums, 'col', 0, 0, tiled=True)]
    gather x1 -> x0, local copies, waits for them, and re-layouts: 2.67 us -> none  [body(): slots = jnp.take(shares.astype(jnp.float16), outgoing, axis=0, mode='clip')]
  transfers between devices with their start and end apart: 38 -> 37, of which waited for: 18 -> 17; matrix products, arithmetic and copies ran while one was open for 3% -> 1% of each run, Pallas kernels for 3% -> 3%
where the time goes in v3:
time: 214 us; the launch traced here: 213 us
  waiting for transfers between devices  110 us (51%)
  starting transfers between devices  50.7 us (24%)
  Pallas kernels  20.7 us (10%)
  local copies, waits for them, and re-layouts  18.5 us (9%)
  blocking collectives  10 us (5%)
  other arithmetic  2.46 us (1%)
    ppermute x34, waiting for transfers between devices, send(): return lax.ppermute(x, AXES, pairs)  93.3 us
    ppermute x34, starting transfers between devices, send(): return lax.ppermute(x, AXES, pairs)  37.1 us
    unnamed x45, local copies, waits for them, and re-layouts  14 us
    all_to_all x1, waiting for transfers between devices, body(): inv = lax.all_to_all(inv, 'col', 0, 0, tiled=True).reshape(NC, COLS)  14 us
    all_to_all x1, blocking collectives, body(): sums = lax.all_to_all(sums, 'col', 0, 0, tiled=True)  10 us
    pallas_call x1, Pallas kernels, late_product(): pl.pallas_call(late_kernel, in_specs=[smem] * 3 + [vmem] * 4 + [anywhere]...  8.46 us
    pallas_call x1, Pallas kernels, early_product(): pl.pallas_call(early_kernel, in_specs=[smem] * 4 + [vmem] + [anywhere] *...  6.96 us
    all_to_all x1, starting transfers between devices, body(): d = jnp.sum(lax.all_to_all(every, 'row', 0, 0, tiled=True), axis=0)  6.74 us
  transfers between devices with their start and end apart: 37, of which 17 were waited for; matrix products, arithmetic and copies ran while one was open for 1% of the time, Pallas kernels for 3%

profile of v3, /device:TPU:0, one launch (start us, length us, event | category | flops | bytes accessed | tf_op | source)
XLA Modules:
  0.0 212.6 jit_solution(6600284998153636035)
XLA Ops:
  0.0 3.9 %shard_map.46 = (bf16[512,1024]{1,0:T(8,128)(2,1)}, f32[16,8,128]{2,1,0:T(8,128)}) custom-call(s32[1]{0:T(128)} %bitcast.6.dev, s32[64,64]{1,0:T(8,128)} %pattern_ref.1, f32[512,1024]{1,0:T(8,128)} %v_ref.1), custom_call_target="tpu_custom_call" | custom-call | tf_op jit(solution)/shard_map/pallas_call | solution.py:88
  6.9 2.7 %collective-permute-start.11 = (bf16[512,1024]{1,0:T(8,128)(2,1)S(1)}, bf16[512,1024]{1,0:T(8,128)(2,1)S(1)}, u32[]{:S(2)}, u32[]{:S(2)}) collective-permute-start(bf16[512,1024]{1,0:T(8,128)(2,1)S(1)} %copy-done), channel_id=1, source_target_pairs={{0,64},{1,65},{2,66},{3,67},{4,68},{5,69},{6,70},{7,71},{8,72},{9,... | collective-permute-start | bytes 3145736 | tf_op jit(solution)/shard_map/ppermute | solution.py:58
  11.6 1.9 collective-permute-start
  13.6 6.5 %collective-permute-done.15.refs_0_ = bf16[256,1024]{1,0:T(8,128)(2,1)S(1)} collective-permute-done((bf16[256,1024]{1,0:T(8,128)(2,1)S(1)}, bf16[256,1024]{1,0:T(8,128)(2,1)S(1)}, u32[]{:S(2)}, u32[]{:S(2)}) %collective-permute-start.15) | collective-permute-done | bytes 524320 | tf_op jit(solution)/shard_map/ppermute | solution.py:58
  21.7 30.8 %collective-permute-done.16.refs_1_ = bf16[256,1024]{1,0:T(8,128)(2,1)S(1)} collective-permute-done((bf16[256,1024]{1,0:T(8,128)(2,1)S(1)}, bf16[256,1024]{1,0:T(8,128)(2,1)S(1)}, u32[]{:S(2)}, u32[]{:S(2)}) %collective-permute-start.16) | collective-permute-done | bytes 524320 | tf_op jit(solution)/shard_map/ppermute | solution.py:58
  53.0 2.2 %collective-permute-start.17 = (bf16[256,1024]{1,0:T(8,128)(2,1)S(1)}, bf16[256,1024]{1,0:T(8,128)(2,1)S(1)}, u32[]{:S(2)}, u32[]{:S(2)}) collective-permute-start(bf16[256,1024]{1,0:T(8,128)(2,1)S(1)} %collective-permute-done.15.refs_0_), channel_id=1, source_target_pairs={{0,2},{1,3},{2,4},{3,5},{4,6},{5,7},{6,0},{7,1},{8,14},{9,15},{10,... | collective-permute-start | bytes 1572872 | tf_op jit(solution)/shard_map/ppermute | solution.py:58
  62.0 2.5 %collective-permute-done.17.refs_2_ = bf16[256,1024]{1,0:T(8,128)(2,1)S(1)} collective-permute-done((bf16[256,1024]{1,0:T(8,128)(2,1)S(1)}, bf16[256,1024]{1,0:T(8,128)(2,1)S(1)}, u32[]{:S(2)}, u32[]{:S(2)}) %collective-permute-start.17) | collective-permute-done | bytes 524320 | tf_op jit(solution)/shard_map/ppermute | solution.py:58
  65.3 4.8 %collective-permute-done.18.refs_3_ = bf16[256,1024]{1,0:T(8,128)(2,1)S(1)} collective-permute-done((bf16[256,1024]{1,0:T(8,128)(2,1)S(1)}, bf16[256,1024]{1,0:T(8,128)(2,1)S(1)}, u32[]{:S(2)}, u32[]{:S(2)}) %collective-permute-start.18) | collective-permute-done | bytes 524320 | tf_op jit(solution)/shard_map/ppermute | solution.py:58
  72.5 3.3 %collective-permute-done.20 = bf16[256,1024]{1,0:T(8,128)(2,1)S(1)} collective-permute-done((bf16[256,1024]{1,0:T(8,128)(2,1)S(1)}, bf16[256,1024]{1,0:T(8,128)(2,1)S(1)}, u32[]{:S(2)}, u32[]{:S(2)}) %collective-permute-start.20) | collective-permute-done | bytes 524320 | tf_op jit(solution)/shard_map/ppermute | solution.py:58
  77.3 4.1 %collective-permute-done.23 = bf16[256,1024]{1,0:T(8,128)(2,1)} collective-permute-done((bf16[256,1024]{1,0:T(8,128)(2,1)S(1)}, bf16[256,1024]{1,0:T(8,128)(2,1)}, u32[]{:S(2)}, u32[]{:S(2)}) %collective-permute-start.23) | collective-permute-done | bytes 524320 | tf_op jit(solution)/shard_map/ppermute | solution.py:58
  87.8 10.4 %collective-permute-done.6.refs_7_ = bf16[512,1024]{1,0:T(8,128)(2,1)} collective-permute-done((bf16[512,1024]{1,0:T(8,128)(2,1)S(1)}, bf16[512,1024]{1,0:T(8,128)(2,1)}, u32[]{:S(2)}, u32[]{:S(2)}) %collective-permute-start.6) | collective-permute-done | bytes 1048608 | tf_op jit(solution)/shard_map/ppermute | solution.py:58
  98.8 9.9 %collective-permute-done.4.refs_3_ = bf16[512,1024]{1,0:T(8,128)(2,1)S(1)} collective-permute-done((bf16[512,1024]{1,0:T(8,128)(2,1)S(1)}, bf16[512,1024]{1,0:T(8,128)(2,1)S(1)}, u32[]{:S(2)}, u32[]{:S(2)}) %collective-permute-start.4) | collective-permute-done | bytes 1048608 | tf_op jit(solution)/shard_map/ppermute | solution.py:58
  114.1 6.7 %all-to-all-start = ((f32[16,8,128]{2,1,0:T(8,128)}), f32[16,8,128]{2,1,0:T(8,128)S(1)}, u32[]{:S(2)}, u32[]{:S(2)}) async-start(f32[16,8,128]{2,1,0:T(8,128)} %get-tuple-element.14), calls=%async_computation | async-start | bytes 131072 | tf_op jit(solution)/shard_map/all_to_all | solution.py:321
  122.1 3.0 %collective-permute-done.28.refs_13_ = bf16[512,1024]{1,0:T(8,128)(2,1)} collective-permute-done((bf16[512,1024]{1,0:T(8,128)(2,1)}, bf16[512,1024]{1,0:T(8,128)(2,1)}, u32[]{:S(2)}, u32[]{:S(2)}) %collective-permute-start.28) | collective-permute-done | bytes 1048608 | tf_op jit(solution)/shard_map/ppermute | solution.py:58
  126.1 2.5 %all-to-all-done = f32[16,8,128]{2,1,0:T(8,128)S(1)} async-done(((f32[16,8,128]{2,1,0:T(8,128)}), f32[16,8,128]{2,1,0:T(8,128)S(1)}, u32[]{:S(2)}, u32[]{:S(2)}) %all-to-all-start) | async-done | bytes 65568 | tf_op jit(solution)/shard_map/all_to_all | solution.py:321
  129.2 3.3 %all-to-all-start.1 = ((f32[8,8,128]{2,1,0:T(8,128)}), f32[8,8,128]{2,1,0:T(8,128)S(1)}, u32[]{:S(2)}, u32[]{:S(2)}) async-start(f32[8,8,128]{2,1,0:T(8,128)} %broadcast_in_dim.28), calls=%async_computation.1 | async-start | bytes 65536 | tf_op jit(solution)/shard_map/all_to_all | solution.py:332
  133.5 14.0 %all-to-all-done.1 = f32[8,8,128]{2,1,0:T(8,128)S(1)} async-done(((f32[8,8,128]{2,1,0:T(8,128)}), f32[8,8,128]{2,1,0:T(8,128)S(1)}, u32[]{:S(2)}, u32[]{:S(2)}) %all-to-all-start.1) | async-done | bytes 32800 | tf_op jit(solution)/shard_map/all_to_all | solution.py:332
  153.6 7.0 %shard_map.47 = (bf16[4,512,1024]{2,1,0:T(8,128)(2,1)S(1)}, bf16[4,1024,1024]{2,1,0:T(8,128)(2,1)S(1)}, f32[512,1024]{1,0:T(8,128)S(1)}) custom-call(s32[5]{0:T(128)S(1)} %stack.23.meta, s32[32]{0:T(128)S(1)} %reshape.114.keep, s32[8]{0:T(128)S(1)} %add_bitcast_fusion.outgoing.slots, s32[8]{0:T(128)S(1)} %select_reduce_fusion.incoming, ...), custom_call_target="tpu_custom_call" | custom-call | tf_op jit(solution)/shard_map/pallas_call | solution.py:167
  160.7 8.5 %shard_map.48 = (f32[16,512,128]{2,1,0:T(8,128)S(1)}, f32[16,128]{1,0:T(8,128)S(1)}) custom-call(s32[5]{0:T(128)S(1)} %stack.23.meta, s32[32]{0:T(128)S(1)} %reshape.114.keep, s32[8]{0:T(128)S(1)} %add_bitcast_fusion.outgoing.slots, f32[8,1024]{1,0:T(8,128)S(1)} %bitcast.15, bf16[4,512,1024]{2,1,0:T(8,128)(2,1)S(1)} %get-tuple-element.16.ae_ref, ...), custom_call_target="tpu_custom_call" | custom-call | tf_op jit(solution)/shard_map/pallas_call | solution.py:246
  170.9 10.0 %all_to_all.27 = f32[8,2,128]{2,1,0:T(2,128)S(1)} all-to-all(f32[8,2,128]{2,1,0:T(2,128)S(1)} %bitcast.16), channel_id=1, replica_groups=mesh['row'=16,'col'=8] {'col'}, dimensions={0} | all-to-all | bytes 16384 | tf_op jit(solution)/shard_map/all_to_all | solution.py:354
  180.9 3.6 %all-to-all-start.2 = ((f16[16,512,128]{2,1,0:T(8,128)(2,1)}), f16[16,512,128]{2,1,0:T(8,128)(2,1)S(1)}, u32[]{:S(2)}, u32[]{:S(2)}) async-start(f16[16,512,128]{2,1,0:T(8,128)(2,1)} %convert_element_type.6), calls=%async_computation.2 | async-start | bytes 4194304 | tf_op jit(solution)/shard_map/all_to_all | solution.py:355
  190.0 3.4 %collective-permute-start.32 = (f32[8,128]{1,0:T(8,128)S(1)}, f32[8,128]{1,0:T(8,128)S(1)}, u32[]{:S(2)}, u32[]{:S(2)}) collective-permute-start(f32[8,128]{1,0:T(8,128)S(1)} %add.72), channel_id=1, source_target_pairs={{0,32},{1,33},{2,34},{3,35},{4,36},{5,37},{6,38},{7,39},{8,40},{9,... | collective-permute-start | bytes 12296 | tf_op jit(solution)/shard_map/ppermute | solution.py:58
  195.1 4.0 %collective-permute-start.33 = (f32[8,128]{1,0:T(8,128)S(1)}, f32[8,128]{1,0:T(8,128)S(1)}, u32[]{:S(2)}, u32[]{:S(2)}) collective-permute-start(f32[8,128]{1,0:T(8,128)S(1)} %add.73), channel_id=1, source_target_pairs={{0,64},{1,65},{2,66},{3,67},{4,68},{5,69},{6,70},{7,71},{8,72},{9,... | collective-permute-start | bytes 12296 | tf_op jit(solution)/shard_map/ppermute | solution.py:58
  199.1 10.8 %collective-permute-done.33 = f32[8,128]{1,0:T(8,128)S(1)} collective-permute-done((f32[8,128]{1,0:T(8,128)S(1)}, f32[8,128]{1,0:T(8,128)S(1)}, u32[]{:S(2)}, u32[]{:S(2)}) %collective-permute-start.33) | collective-permute-done | bytes 4128 | tf_op jit(solution)/shard_map/ppermute | solution.py:58
  (125 shorter events, 52.4 us)
Async XLA Ops:
  6.9 45.6 %collective-permute-start.11 = (bf16[512,1024]{1,0:T(8,128)(2,1)S(1)}, bf16[512,1024]{1,0:T(8,128)(2,1)S(1)}, u32[]{:S(2)}, u32[]{:S(2)}) collective-permute-start(bf16[512,1024]{1,0:T(8,128)(2,1)S(1)} %copy-done), channel_id=1, source_target_pairs={{0,64},{1,65},{2,66},{3,67},{4,68},{5,69},{6,70},{7,71},{8,72},{9,... | collective-permute-start | bytes 3145736 | tf_op jit(solution)/shard_map/ppermute | solution.py:58
  9.6 43.4 %collective-permute-start.5 = (bf16[512,1024]{1,0:T(8,128)(2,1)S(1)}, bf16[512,1024]{1,0:T(8,128)(2,1)S(1)}, u32[]{:S(2)}, u32[]{:S(2)}) collective-permute-start(bf16[512,1024]{1,0:T(8,128)(2,1)S(1)} %copy-done), channel_id=1, source_target_pairs={{0,16},{1,17},{2,18},{3,19},{4,20},{5,21},{6,22},{7,23},{8,56},{9,... | collective-permute-start | bytes 3145736 | tf_op jit(solution)/shard_map/ppermute | solution.py:58
  11.2 44.8 %collective-permute-start.1 = (bf16[512,1024]{1,0:T(8,128)(2,1)S(1)}, bf16[512,1024]{1,0:T(8,128)(2,1)S(1)}, u32[]{:S(2)}, u32[]{:S(2)}) collective-permute-start(bf16[512,1024]{1,0:T(8,128)(2,1)S(1)} %copy-done), channel_id=1, source_target_pairs={{0,8},{1,9},{2,10},{3,11},{4,12},{5,13},{6,14},{7,15},{8,0},{9,1},... | collective-permute-start | bytes 3145736 | tf_op jit(solution)/shard_map/ppermute | solution.py:58
  11.6 46.3 %collective-permute-start = (bf16[512,1024]{1,0:T(8,128)(2,1)S(1)}, bf16[512,1024]{1,0:T(8,128)(2,1)S(1)}, u32[]{:S(2)}, u32[]{:S(2)}) collective-permute-start(bf16[512,1024]{1,0:T(8,128)(2,1)S(1)} %copy-done), channel_id=1, source_target_pairs={{0,2},{1,3},{2,4},{3,5},{4,6},{5,7},{6,0},{7,1},{8,14},{9,15},{10,... | collective-permute-start | bytes 3145736 | tf_op jit(solution)/shard_map/ppermute | solution.py:58
  20.1 32.4 %collective-permute-start.16 = (bf16[256,1024]{1,0:T(8,128)(2,1)S(1)}, bf16[256,1024]{1,0:T(8,128)(2,1)S(1)}, u32[]{:S(2)}, u32[]{:S(2)}) collective-permute-start(bf16[256,1024]{1,0:T(8,128)(2,1)S(1)} %get-tuple-element.23), channel_id=1, source_target_pairs={{0,1},{1,0},{2,3},{3,2},{4,5},{5,4},{6,7},{7,6},{8,9},{9,8},{10,11... | collective-permute-start | bytes 1572872 | tf_op jit(solution)/shard_map/ppermute | solution.py:58
  56.0 26.4 %collective-permute-start.12 = (bf16[512,1024]{1,0:T(8,128)(2,1)S(1)}, bf16[512,1024]{1,0:T(8,128)(2,1)S(1)}, u32[]{:S(2)}, u32[]{:S(2)}) collective-permute-start(bf16[512,1024]{1,0:T(8,128)(2,1)S(1)} %collective-permute-done.11.refs_12_.refs_7_), channel_id=1, source_target_pairs={{0,8},{1,9},{2,10},{3,11},{4,12},{5,13},{6,14},{7,15},{8,0},{9,1},... | collective-permute-start | bytes 3145736 | tf_op jit(solution)/shard_map/ppermute | solution.py:58
  57.9 27.3 %collective-permute-start.13 = (bf16[512,1024]{1,0:T(8,128)(2,1)S(1)}, bf16[512,1024]{1,0:T(8,128)(2,1)}, u32[]{:S(2)}, u32[]{:S(2)}) collective-permute-start(bf16[512,1024]{1,0:T(8,128)(2,1)S(1)} %collective-permute-done.11.refs_12_.refs_7_), channel_id=1, source_target_pairs={{0,16},{1,17},{2,18},{3,19},{4,20},{5,21},{6,22},{7,23},{8,56},{9,... | collective-permute-start | bytes 3145736 | tf_op jit(solution)/shard_map/ppermute | solution.py:58
  65.3 16.2 %collective-permute-start.23 = (bf16[256,1024]{1,0:T(8,128)(2,1)S(1)}, bf16[256,1024]{1,0:T(8,128)(2,1)}, u32[]{:S(2)}, u32[]{:S(2)}) collective-permute-start(bf16[256,1024]{1,0:T(8,128)(2,1)S(1)} %collective-permute-done.22), channel_id=1, source_target_pairs={{0,2},{1,3},{2,4},{3,5},{4,6},{5,7},{6,0},{7,1},{8,14},{9,15},{10,... | collective-permute-start | bytes 1572872 | tf_op jit(solution)/shard_map/ppermute | solution.py:58
  70.9 16.1 %collective-permute-start.9 = (bf16[512,1024]{1,0:T(8,128)(2,1)S(1)}, bf16[512,1024]{1,0:T(8,128)(2,1)}, u32[]{:S(2)}, u32[]{:S(2)}) collective-permute-start(bf16[512,1024]{1,0:T(8,128)(2,1)S(1)} %collective-permute-done.5.refs_6_), channel_id=1, source_target_pairs={{0,16},{1,17},{2,18},{3,19},{4,20},{5,21},{6,22},{7,23},{8,56},{9,... | collective-permute-start | bytes 3145736 | tf_op jit(solution)/shard_map/ppermute | solution.py:58
  75.7 22.5 %collective-permute-start.6 = (bf16[512,1024]{1,0:T(8,128)(2,1)S(1)}, bf16[512,1024]{1,0:T(8,128)(2,1)}, u32[]{:S(2)}, u32[]{:S(2)}) collective-permute-start(bf16[512,1024]{1,0:T(8,128)(2,1)S(1)} %collective-permute-done.1.refs_5_), channel_id=1, source_target_pairs={{0,16},{1,17},{2,18},{3,19},{4,20},{5,21},{6,22},{7,23},{8,56},{9,... | collective-permute-start | bytes 3145736 | tf_op jit(solution)/shard_map/ppermute | solution.py:58
  81.5 16.8 %collective-permute-start.2 = (bf16[512,1024]{1,0:T(8,128)(2,1)S(1)}, bf16[512,1024]{1,0:T(8,128)(2,1)}, u32[]{:S(2)}, u32[]{:S(2)}) collective-permute-start(bf16[512,1024]{1,0:T(8,128)(2,1)S(1)} %collective-permute-done.1.refs_5_), channel_id=1, source_target_pairs={{0,2},{1,3},{2,4},{3,5},{4,6},{5,7},{6,0},{7,1},{8,14},{9,15},{10,... | collective-permute-start | bytes 3145736 | tf_op jit(solution)/shard_map/ppermute | solution.py:58
  82.4 26.3 %collective-permute-start.4 = (bf16[512,1024]{1,0:T(8,128)(2,1)S(1)}, bf16[512,1024]{1,0:T(8,128)(2,1)S(1)}, u32[]{:S(2)}, u32[]{:S(2)}) collective-permute-start(bf16[512,1024]{1,0:T(8,128)(2,1)S(1)} %collective-permute-done.refs_1_), channel_id=1, source_target_pairs={{0,2},{1,3},{2,4},{3,5},{4,6},{5,7},{6,0},{7,1},{8,14},{9,15},{10,... | collective-permute-start | bytes 3145736 | tf_op jit(solution)/shard_map/ppermute | solution.py:58
  85.2 25.1 %collective-permute-start.8 = (bf16[512,1024]{1,0:T(8,128)(2,1)S(1)}, bf16[512,1024]{1,0:T(8,128)(2,1)S(1)}, u32[]{:S(2)}, u32[]{:S(2)}) collective-permute-start(bf16[512,1024]{1,0:T(8,128)(2,1)S(1)} %collective-permute-done.5.refs_6_), channel_id=1, source_target_pairs={{0,8},{1,9},{2,10},{3,11},{4,12},{5,13},{6,14},{7,15},{8,0},{9,1},... | collective-permute-start | bytes 3145736 | tf_op jit(solution)/shard_map/ppermute | solution.py:58
  87.0 33.9 %collective-permute-start.14 = (bf16[512,1024]{1,0:T(8,128)(2,1)S(1)}, bf16[512,1024]{1,0:T(8,128)(2,1)}, u32[]{:S(2)}, u32[]{:S(2)}) collective-permute-start(bf16[512,1024]{1,0:T(8,128)(2,1)S(1)} %collective-permute-done.12.refs_13_.refs_8_), channel_id=1, source_target_pairs={{0,16},{1,17},{2,18},{3,19},{4,20},{5,21},{6,22},{7,23},{8,56},{9,... | collective-permute-start | bytes 3145736 | tf_op jit(solution)/shard_map/ppermute | solution.py:58
  98.3 23.2 %collective-permute-start.10 = (bf16[512,1024]{1,0:T(8,128)(2,1)}, bf16[512,1024]{1,0:T(8,128)(2,1)}, u32[]{:S(2)}, u32[]{:S(2)}) collective-permute-start(bf16[512,1024]{1,0:T(8,128)(2,1)} %collective-permute-done.9.refs_10_), channel_id=1, source_target_pairs={{0,8},{1,9},{2,10},{3,11},{4,12},{5,13},{6,14},{7,15},{8,0},{9,1},... | collective-permute-start | bytes 3145736 | tf_op jit(solution)/shard_map/ppermute | solution.py:58
  98.3 23.8 %collective-permute-start.7 = (bf16[512,1024]{1,0:T(8,128)(2,1)}, bf16[512,1024]{1,0:T(8,128)(2,1)}, u32[]{:S(2)}, u32[]{:S(2)}) collective-permute-start(bf16[512,1024]{1,0:T(8,128)(2,1)} %collective-permute-done.6.refs_7_), channel_id=1, source_target_pairs={{0,8},{1,9},{2,10},{3,11},{4,12},{5,13},{6,14},{7,15},{8,0},{9,1},... | collective-permute-start | bytes 3145736 | tf_op jit(solution)/shard_map/ppermute | solution.py:58
  108.7 16.3 %collective-permute-start.28 = (bf16[512,1024]{1,0:T(8,128)(2,1)}, bf16[512,1024]{1,0:T(8,128)(2,1)}, u32[]{:S(2)}, u32[]{:S(2)}) collective-permute-start(bf16[512,1024]{1,0:T(8,128)(2,1)} %collective-permute-done.13.refs_14_.refs_9_), channel_id=1, source_target_pairs={{0,16},{1,17},{2,18},{3,19},{4,20},{5,21},{6,22},{7,23},{8,56},{9,... | collective-permute-start | bytes 3145736 | tf_op jit(solution)/shard_map/ppermute | solution.py:58
  121.0 39.6 %collective-permute-start.27 = (bf16[512,1024]{1,0:T(8,128)(2,1)}, bf16[512,1024]{1,0:T(8,128)(2,1)}, u32[]{:S(2)}, u32[]{:S(2)}) collective-permute-start(bf16[512,1024]{1,0:T(8,128)(2,1)} %collective-permute-done.13.refs_14_.refs_9_), channel_id=1, source_target_pairs={{0,8},{1,9},{2,10},{3,11},{4,12},{5,13},{6,14},{7,15},{8,0},{9,1},... | collective-permute-start | bytes 3145736 | tf_op jit(solution)/shard_map/ppermute | solution.py:58
  121.5 39.1 %collective-permute-start.25 = (bf16[512,1024]{1,0:T(8,128)(2,1)}, bf16[512,1024]{1,0:T(8,128)(2,1)}, u32[]{:S(2)}, u32[]{:S(2)}) collective-permute-start(bf16[512,1024]{1,0:T(8,128)(2,1)} %copy-done.7), channel_id=1, source_target_pairs={{0,1},{1,0},{2,3},{3,2},{4,5},{5,4},{6,7},{7,6},{8,9},{9,8},{10,11... | collective-permute-start | bytes 3145736 | tf_op jit(solution)/shard_map/ppermute | solution.py:58
  122.1 38.5 %collective-permute-start.26 = (bf16[512,1024]{1,0:T(8,128)(2,1)}, bf16[512,1024]{1,0:T(8,128)(2,1)}, u32[]{:S(2)}, u32[]{:S(2)}) collective-permute-start(bf16[512,1024]{1,0:T(8,128)(2,1)} %collective-permute-done.14.refs_15_.refs_10_), channel_id=1, source_target_pairs={{0,8},{1,9},{2,10},{3,11},{4,12},{5,13},{6,14},{7,15},{8,0},{9,1},... | collective-permute-start | bytes 3145736 | tf_op jit(solution)/shard_map/ppermute | solution.py:58
  125.0 35.6 %collective-permute-start.29 = (bf16[512,1024]{1,0:T(8,128)(2,1)}, bf16[512,1024]{1,0:T(8,128)(2,1)}, u32[]{:S(2)}, u32[]{:S(2)}) collective-permute-start(bf16[512,1024]{1,0:T(8,128)(2,1)} %collective-permute-done.28.refs_13_), channel_id=1, source_target_pairs={{0,8},{1,9},{2,10},{3,11},{4,12},{5,13},{6,14},{7,15},{8,0},{9,1},... | collective-permute-start | bytes 3145736 | tf_op jit(solution)/shard_map/ppermute | solution.py:58
  125.2 35.3 %collective-permute-start.24 = (bf16[256,1024]{1,0:T(8,128)(2,1)}, bf16[256,1024]{1,0:T(8,128)(2,1)}, u32[]{:S(2)}, u32[]{:S(2)}) collective-permute-start(bf16[256,1024]{1,0:T(8,128)(2,1)} %collective-permute-done.23), channel_id=1, source_target_pairs={{0,8},{1,9},{2,10},{3,11},{4,12},{5,13},{6,14},{7,15},{8,0},{9,1},... | collective-permute-start | bytes 1572872 | tf_op jit(solution)/shard_map/ppermute | solution.py:58
  129.2 18.3 %all-to-all-start.1 = ((f32[8,8,128]{2,1,0:T(8,128)}), f32[8,8,128]{2,1,0:T(8,128)S(1)}, u32[]{:S(2)}, u32[]{:S(2)}) async-start(f32[8,8,128]{2,1,0:T(8,128)} %broadcast_in_dim.28), calls=%async_computation.1 | async-start | bytes 65536 | tf_op jit(solution)/shard_map/all_to_all | solution.py:332
  180.9 28.9 %all-to-all-start.2 = ((f16[16,512,128]{2,1,0:T(8,128)(2,1)}), f16[16,512,128]{2,1,0:T(8,128)(2,1)S(1)}, u32[]{:S(2)}, u32[]{:S(2)}) async-start(f16[16,512,128]{2,1,0:T(8,128)(2,1)} %convert_element_type.6), calls=%async_computation.2 | async-start | bytes 4194304 | tf_op jit(solution)/shard_map/all_to_all | solution.py:355
  (35 other events, 294.1 us)

commit v4 on v3

--- a/solution.py
+++ b/solution.py
@@ -261,26 +261,26 @@
     )(meta, keep, slots, inv, *early, *a_pieces, *b_pieces)
 
 
-def columns_kernel(x_ref, o_ref, sem):
+def columns_kernel(index, x_ref, o_ref, sem):
     copies = []
     for j in range(NC):
         dst = o_ref.at[:, pl.ds(j * BLK, BLK)]
-        copies.append(pltpu.make_async_copy(x_ref.at[j], dst, sem.at[j]))
+        copies.append(pltpu.make_async_copy(x_ref.at[index[j]], dst, sem.at[j]))
     for copy in copies:
         copy.start()
     for copy in copies:
         copy.wait()
 
 
-def side_by_side(blocks):
+def side_by_side(index, blocks):
     return pl.pallas_call(
         columns_kernel,
-        in_specs=[pl.BlockSpec(memory_space=pltpu.VMEM)],
+        in_specs=[pl.BlockSpec(memory_space=pltpu.SMEM), pl.BlockSpec(memory_space=pltpu.VMEM)],
         out_specs=pl.BlockSpec(memory_space=pltpu.HBM),
         out_shape=jax.ShapeDtypeStruct((ROWS, COLS), jnp.float32),
         scratch_shapes=[pltpu.SemaphoreType.DMA((NC,))],
         compiler_params=pltpu.CompilerParams(vmem_limit_bytes=LAST_LIMIT),
-    )(pltpu.with_memory_space_constraint(blocks, pltpu.VMEM))
+    )(index, pltpu.with_memory_space_constraint(blocks, pltpu.VMEM))
 
 
 def slot_tables(owners, me_col):
@@ -353,14 +353,13 @@
     slots, sums = lax.optimization_barrier((shares.astype(jnp.float16), sums))
     sums = lax.all_to_all(sums, "col", 0, 0, tiled=True)
     arrived = lax.all_to_all(slots, "col", 0, 0, tiled=True)
-    sums = jnp.take(sums, incoming, axis=0, mode="clip")
     total = sums + send(sums, core)
     total = total + send(total, ring_xor(1))
     total = total + send(total, ring_xor(2))
     total = total + send(total, flip("xh"))
     weight = sums / total * jnp.float32(NR)
-    placed = jnp.take(arrived, incoming, axis=0, mode="clip")
-    return side_by_side(placed.astype(jnp.float32) * weight[:, None, :])
+    placed = arrived.astype(jnp.float32) * weight[:, None, :]
+    return side_by_side(incoming, placed)
 
 
 def solution(mesh):

time: 214 us -> 215 us (level)
    unnamed x45 -> x47, local copies, waits for them, and re-layouts: 14 us -> 16.1 us
  transfers between devices with their start and end apart: 37 -> 37, of which waited for: 17 -> 16; matrix products, arithmetic and copies ran while one was open for 1% -> 1% of each run, Pallas kernels for 3% -> 3%
where the time goes in v4:
time: 215 us; the launch traced here: 213 us
  waiting for transfers between devices  109 us (51%)
  starting transfers between devices  51.2 us (24%)
  Pallas kernels  21.2 us (10%)
  local copies, waits for them, and re-layouts  19.1 us (9%)
  blocking collectives  10 us (5%)
  other arithmetic  2.64 us (1%)
    ppermute x34, waiting for transfers between devices, send(): return lax.ppermute(x, AXES, pairs)  92.3 us
    ppermute x34, starting transfers between devices, send(): return lax.ppermute(x, AXES, pairs)  37.5 us
    unnamed x47, local copies, waits for them, and re-layouts  16.1 us
    all_to_all x1, waiting for transfers between devices, body(): inv = lax.all_to_all(inv, 'col', 0, 0, tiled=True).reshape(NC, COLS)  13.9 us
    all_to_all x1, blocking collectives, body(): sums = lax.all_to_all(sums, 'col', 0, 0, tiled=True)  10 us
    pallas_call x1, Pallas kernels, late_product(): pl.pallas_call(late_kernel, in_specs=[smem] * 3 + [vmem] * 4 + [anywhere]...  8.47 us
    pallas_call x1, Pallas kernels, early_product(): pl.pallas_call(early_kernel, in_specs=[smem] * 4 + [vmem] + [anywhere] *...  6.96 us
    all_to_all x1, starting transfers between devices, body(): d = jnp.sum(lax.all_to_all(every, 'row', 0, 0, tiled=True), axis=0)  6.74 us
  transfers between devices with their start and end apart: 37, of which 16 were waited for; matrix products, arithmetic and copies ran while one was open for 1% of the time, Pallas kernels for 3%

profile of v4, /device:TPU:0, one launch (start us, length us, event | category | flops | bytes accessed | tf_op | source)
XLA Modules:
  0.0 213.5 jit_solution(11953816247420985664)
XLA Ops:
  0.0 3.9 %shard_map.46 = (bf16[512,1024]{1,0:T(8,128)(2,1)}, f32[16,8,128]{2,1,0:T(8,128)}) custom-call(s32[1]{0:T(128)} %bitcast.6.dev, s32[64,64]{1,0:T(8,128)} %pattern_ref.1, f32[512,1024]{1,0:T(8,128)} %v_ref.1), custom_call_target="tpu_custom_call" | custom-call | tf_op jit(solution)/shard_map/pallas_call | solution.py:88
  6.8 2.7 %collective-permute-start.11 = (bf16[512,1024]{1,0:T(8,128)(2,1)}, bf16[512,1024]{1,0:T(8,128)(2,1)S(1)}, u32[]{:S(2)}, u32[]{:S(2)}) collective-permute-start(bf16[512,1024]{1,0:T(8,128)(2,1)} %get-tuple-element.15.refs_0_.refs_4_), channel_id=1, source_target_pairs={{0,64},{1,65},{2,66},{3,67},{4,68},{5,69},{6,70},{7,71},{8,72},{9,... | collective-permute-start | bytes 3145736 | tf_op jit(solution)/shard_map/ppermute | solution.py:58
  13.5 6.5 %collective-permute-done.15.refs_0_ = bf16[256,1024]{1,0:T(8,128)(2,1)S(1)} collective-permute-done((bf16[256,1024]{1,0:T(8,128)(2,1)S(1)}, bf16[256,1024]{1,0:T(8,128)(2,1)S(1)}, u32[]{:S(2)}, u32[]{:S(2)}) %collective-permute-start.15) | collective-permute-done | bytes 524320 | tf_op jit(solution)/shard_map/ppermute | solution.py:58
  21.6 30.8 %collective-permute-done.16.refs_1_ = bf16[256,1024]{1,0:T(8,128)(2,1)S(1)} collective-permute-done((bf16[256,1024]{1,0:T(8,128)(2,1)S(1)}, bf16[256,1024]{1,0:T(8,128)(2,1)S(1)}, u32[]{:S(2)}, u32[]{:S(2)}) %collective-permute-start.16) | collective-permute-done | bytes 524320 | tf_op jit(solution)/shard_map/ppermute | solution.py:58
  53.0 2.2 %collective-permute-start.17 = (bf16[256,1024]{1,0:T(8,128)(2,1)S(1)}, bf16[256,1024]{1,0:T(8,128)(2,1)S(1)}, u32[]{:S(2)}, u32[]{:S(2)}) collective-permute-start(bf16[256,1024]{1,0:T(8,128)(2,1)S(1)} %collective-permute-done.15.refs_0_), channel_id=1, source_target_pairs={{0,2},{1,3},{2,4},{3,5},{4,6},{5,7},{6,0},{7,1},{8,14},{9,15},{10,... | collective-permute-start | bytes 1572872 | tf_op jit(solution)/shard_map/ppermute | solution.py:58
  61.9 2.5 %collective-permute-done.17.refs_2_ = bf16[256,1024]{1,0:T(8,128)(2,1)S(1)} collective-permute-done((bf16[256,1024]{1,0:T(8,128)(2,1)S(1)}, bf16[256,1024]{1,0:T(8,128)(2,1)S(1)}, u32[]{:S(2)}, u32[]{:S(2)}) %collective-permute-start.17) | collective-permute-done | bytes 524320 | tf_op jit(solution)/shard_map/ppermute | solution.py:58
  65.2 4.8 %collective-permute-done.18.refs_3_ = bf16[256,1024]{1,0:T(8,128)(2,1)S(1)} collective-permute-done((bf16[256,1024]{1,0:T(8,128)(2,1)S(1)}, bf16[256,1024]{1,0:T(8,128)(2,1)S(1)}, u32[]{:S(2)}, u32[]{:S(2)}) %collective-permute-start.18) | collective-permute-done | bytes 524320 | tf_op jit(solution)/shard_map/ppermute | solution.py:58
  72.4 3.2 %collective-permute-done.20 = bf16[256,1024]{1,0:T(8,128)(2,1)S(1)} collective-permute-done((bf16[256,1024]{1,0:T(8,128)(2,1)S(1)}, bf16[256,1024]{1,0:T(8,128)(2,1)S(1)}, u32[]{:S(2)}, u32[]{:S(2)}) %collective-permute-start.20) | collective-permute-done | bytes 524320 | tf_op jit(solution)/shard_map/ppermute | solution.py:58
  77.2 4.0 %collective-permute-done.23 = bf16[256,1024]{1,0:T(8,128)(2,1)S(1)} collective-permute-done((bf16[256,1024]{1,0:T(8,128)(2,1)S(1)}, bf16[256,1024]{1,0:T(8,128)(2,1)S(1)}, u32[]{:S(2)}, u32[]{:S(2)}) %collective-permute-start.23) | collective-permute-done | bytes 524320 | tf_op jit(solution)/shard_map/ppermute | solution.py:58
  88.5 9.6 %collective-permute-done.6.refs_7_ = bf16[512,1024]{1,0:T(8,128)(2,1)} collective-permute-done((bf16[512,1024]{1,0:T(8,128)(2,1)S(1)}, bf16[512,1024]{1,0:T(8,128)(2,1)}, u32[]{:S(2)}, u32[]{:S(2)}) %collective-permute-start.6) | collective-permute-done | bytes 1048608 | tf_op jit(solution)/shard_map/ppermute | solution.py:58
  98.7 9.8 %collective-permute-done.4.refs_3_ = bf16[512,1024]{1,0:T(8,128)(2,1)S(1)} collective-permute-done((bf16[512,1024]{1,0:T(8,128)(2,1)S(1)}, bf16[512,1024]{1,0:T(8,128)(2,1)S(1)}, u32[]{:S(2)}, u32[]{:S(2)}) %collective-permute-start.4) | collective-permute-done | bytes 1048608 | tf_op jit(solution)/shard_map/ppermute | solution.py:58
  113.9 6.7 %all-to-all-start = ((f32[16,8,128]{2,1,0:T(8,128)}), f32[16,8,128]{2,1,0:T(8,128)S(1)}, u32[]{:S(2)}, u32[]{:S(2)}) async-start(f32[16,8,128]{2,1,0:T(8,128)} %get-tuple-element.14), calls=%async_computation | async-start | bytes 131072 | tf_op jit(solution)/shard_map/all_to_all | solution.py:321
  121.9 2.8 %collective-permute-done.28.refs_13_ = bf16[512,1024]{1,0:T(8,128)(2,1)} collective-permute-done((bf16[512,1024]{1,0:T(8,128)(2,1)S(1)}, bf16[512,1024]{1,0:T(8,128)(2,1)}, u32[]{:S(2)}, u32[]{:S(2)}) %collective-permute-start.28) | collective-permute-done | bytes 1048608 | tf_op jit(solution)/shard_map/ppermute | solution.py:58
  125.7 2.7 %all-to-all-done = f32[16,8,128]{2,1,0:T(8,128)S(1)} async-done(((f32[16,8,128]{2,1,0:T(8,128)}), f32[16,8,128]{2,1,0:T(8,128)S(1)}, u32[]{:S(2)}, u32[]{:S(2)}) %all-to-all-start) | async-done | bytes 65568 | tf_op jit(solution)/shard_map/all_to_all | solution.py:321
  129.0 3.3 %all-to-all-start.1 = ((f32[8,8,128]{2,1,0:T(8,128)}), f32[8,8,128]{2,1,0:T(8,128)S(1)}, u32[]{:S(2)}, u32[]{:S(2)}) async-start(f32[8,8,128]{2,1,0:T(8,128)} %broadcast_in_dim.23), calls=%async_computation.1 | async-start | bytes 65536 | tf_op jit(solution)/shard_map/all_to_all | solution.py:332
  133.3 13.9 %all-to-all-done.1 = f32[8,8,128]{2,1,0:T(8,128)S(1)} async-done(((f32[8,8,128]{2,1,0:T(8,128)}), f32[8,8,128]{2,1,0:T(8,128)S(1)}, u32[]{:S(2)}, u32[]{:S(2)}) %all-to-all-start.1) | async-done | bytes 32800 | tf_op jit(solution)/shard_map/all_to_all | solution.py:332
  154.6 7.0 %shard_map.47 = (bf16[4,512,1024]{2,1,0:T(8,128)(2,1)S(1)}, bf16[4,1024,1024]{2,1,0:T(8,128)(2,1)S(1)}, f32[512,1024]{1,0:T(8,128)S(1)}) custom-call(s32[5]{0:T(128)S(1)} %stack.23.meta, s32[32]{0:T(128)S(1)} %reshape.112.keep, s32[8]{0:T(128)S(1)} %add_bitcast_fusion.outgoing.slots, s32[8]{0:T(128)S(1)} %select_reduce_fusion.incoming.index, ...), custom_call_target="tpu_custom_call" | custom-call | tf_op jit(solution)/shard_map/pallas_call | solution.py:167
  161.7 8.5 %shard_map.48 = (f32[16,512,128]{2,1,0:T(8,128)S(1)}, f32[16,128]{1,0:T(8,128)S(1)}) custom-call(s32[5]{0:T(128)S(1)} %stack.23.meta, s32[32]{0:T(128)S(1)} %reshape.112.keep, s32[8]{0:T(128)S(1)} %add_bitcast_fusion.outgoing.slots, f32[8,1024]{1,0:T(8,128)S(1)} %bitcast.15, bf16[4,512,1024]{2,1,0:T(8,128)(2,1)S(1)} %get-tuple-element.16.ae_ref, ...), custom_call_target="tpu_custom_call" | custom-call | tf_op jit(solution)/shard_map/pallas_call | solution.py:246
  171.9 10.0 %all_to_all.27 = f32[8,2,128]{2,1,0:T(2,128)S(1)} all-to-all(f32[8,2,128]{2,1,0:T(2,128)S(1)} %bitcast.16), channel_id=1, replica_groups=mesh['row'=16,'col'=8] {'col'}, dimensions={0} | all-to-all | bytes 16384 | tf_op jit(solution)/shard_map/all_to_all | solution.py:354
  182.0 3.6 %all-to-all-start.2 = ((f16[16,512,128]{2,1,0:T(8,128)(2,1)}), f16[16,512,128]{2,1,0:T(8,128)(2,1)S(1)}, u32[]{:S(2)}, u32[]{:S(2)}) async-start(f16[16,512,128]{2,1,0:T(8,128)(2,1)} %convert_element_type.6), calls=%async_computation.2 | async-start | bytes 4194304 | tf_op jit(solution)/shard_map/all_to_all | solution.py:355
  190.5 3.4 %collective-permute-start.32 = (f32[16,128]{1,0:T(8,128)S(1)}, f32[16,128]{1,0:T(8,128)S(1)}, u32[]{:S(2)}, u32[]{:S(2)}) collective-permute-start(f32[16,128]{1,0:T(8,128)S(1)} %add.72), channel_id=1, source_target_pairs={{0,32},{1,33},{2,34},{3,35},{4,36},{5,37},{6,38},{7,39},{8,40},{9,... | collective-permute-start | bytes 24584 | tf_op jit(solution)/shard_map/ppermute | solution.py:58
  195.7 4.0 %collective-permute-start.33 = (f32[16,128]{1,0:T(8,128)S(1)}, f32[16,128]{1,0:T(8,128)S(1)}, u32[]{:S(2)}, u32[]{:S(2)}) collective-permute-start(f32[16,128]{1,0:T(8,128)S(1)} %add.73), channel_id=1, source_target_pairs={{0,64},{1,65},{2,66},{3,67},{4,68},{5,69},{6,70},{7,71},{8,72},{9,... | collective-permute-start | bytes 24584 | tf_op jit(solution)/shard_map/ppermute | solution.py:58
  199.6 11.4 %collective-permute-done.33 = f32[16,128]{1,0:T(8,128)S(1)} collective-permute-done((f32[16,128]{1,0:T(8,128)S(1)}, f32[16,128]{1,0:T(8,128)S(1)}, u32[]{:S(2)}, u32[]{:S(2)}) %collective-permute-start.33) | collective-permute-done | bytes 8224 | tf_op jit(solution)/shard_map/ppermute | solution.py:58
  211.4 1.9 shard_map.49
  (124 shorter events, 53.7 us)
Async XLA Ops:
  6.8 45.6 %collective-permute-start.11 = (bf16[512,1024]{1,0:T(8,128)(2,1)}, bf16[512,1024]{1,0:T(8,128)(2,1)S(1)}, u32[]{:S(2)}, u32[]{:S(2)}) collective-permute-start(bf16[512,1024]{1,0:T(8,128)(2,1)} %get-tuple-element.15.refs_0_.refs_4_), channel_id=1, source_target_pairs={{0,64},{1,65},{2,66},{3,67},{4,68},{5,69},{6,70},{7,71},{8,72},{9,... | collective-permute-start | bytes 3145736 | tf_op jit(solution)/shard_map/ppermute | solution.py:58
  9.6 43.4 %collective-permute-start.5 = (bf16[512,1024]{1,0:T(8,128)(2,1)}, bf16[512,1024]{1,0:T(8,128)(2,1)S(1)}, u32[]{:S(2)}, u32[]{:S(2)}) collective-permute-start(bf16[512,1024]{1,0:T(8,128)(2,1)} %get-tuple-element.15.refs_0_.refs_4_), channel_id=1, source_target_pairs={{0,16},{1,17},{2,18},{3,19},{4,20},{5,21},{6,22},{7,23},{8,56},{9,... | collective-permute-start | bytes 3145736 | tf_op jit(solution)/shard_map/ppermute | solution.py:58
  11.1 44.8 %collective-permute-start.1 = (bf16[512,1024]{1,0:T(8,128)(2,1)}, bf16[512,1024]{1,0:T(8,128)(2,1)S(1)}, u32[]{:S(2)}, u32[]{:S(2)}) collective-permute-start(bf16[512,1024]{1,0:T(8,128)(2,1)} %get-tuple-element.15.refs_0_.refs_4_), channel_id=1, source_target_pairs={{0,8},{1,9},{2,10},{3,11},{4,12},{5,13},{6,14},{7,15},{8,0},{9,1},... | collective-permute-start | bytes 3145736 | tf_op jit(solution)/shard_map/ppermute | solution.py:58
  11.6 46.3 %collective-permute-start = (bf16[512,1024]{1,0:T(8,128)(2,1)}, bf16[512,1024]{1,0:T(8,128)(2,1)S(1)}, u32[]{:S(2)}, u32[]{:S(2)}) collective-permute-start(bf16[512,1024]{1,0:T(8,128)(2,1)} %get-tuple-element.15.refs_0_.refs_4_), channel_id=1, source_target_pairs={{0,2},{1,3},{2,4},{3,5},{4,6},{5,7},{6,0},{7,1},{8,14},{9,15},{10,... | collective-permute-start | bytes 3145736 | tf_op jit(solution)/shard_map/ppermute | solution.py:58
  20.0 32.4 %collective-permute-start.16 = (bf16[256,1024]{1,0:T(8,128)(2,1)S(1)}, bf16[256,1024]{1,0:T(8,128)(2,1)S(1)}, u32[]{:S(2)}, u32[]{:S(2)}) collective-permute-start(bf16[256,1024]{1,0:T(8,128)(2,1)S(1)} %get-tuple-element.23), channel_id=1, source_target_pairs={{0,1},{1,0},{2,3},{3,2},{4,5},{5,4},{6,7},{7,6},{8,9},{9,8},{10,11... | collective-permute-start | bytes 1572872 | tf_op jit(solution)/shard_map/ppermute | solution.py:58
  55.9 27.1 %collective-permute-start.12 = (bf16[512,1024]{1,0:T(8,128)(2,1)S(1)}, bf16[512,1024]{1,0:T(8,128)(2,1)S(1)}, u32[]{:S(2)}, u32[]{:S(2)}) collective-permute-start(bf16[512,1024]{1,0:T(8,128)(2,1)S(1)} %collective-permute-done.11.refs_12_.refs_7_), channel_id=1, source_target_pairs={{0,8},{1,9},{2,10},{3,11},{4,12},{5,13},{6,14},{7,15},{8,0},{9,1},... | collective-permute-start | bytes 3145736 | tf_op jit(solution)/shard_map/ppermute | solution.py:58
  57.9 27.3 %collective-permute-start.13 = (bf16[512,1024]{1,0:T(8,128)(2,1)S(1)}, bf16[512,1024]{1,0:T(8,128)(2,1)S(1)}, u32[]{:S(2)}, u32[]{:S(2)}) collective-permute-start(bf16[512,1024]{1,0:T(8,128)(2,1)S(1)} %collective-permute-done.11.refs_12_.refs_7_), channel_id=1, source_target_pairs={{0,16},{1,17},{2,18},{3,19},{4,20},{5,21},{6,22},{7,23},{8,56},{9,... | collective-permute-start | bytes 3145736 | tf_op jit(solution)/shard_map/ppermute | solution.py:58
  65.2 16.1 %collective-permute-start.23 = (bf16[256,1024]{1,0:T(8,128)(2,1)S(1)}, bf16[256,1024]{1,0:T(8,128)(2,1)S(1)}, u32[]{:S(2)}, u32[]{:S(2)}) collective-permute-start(bf16[256,1024]{1,0:T(8,128)(2,1)S(1)} %collective-permute-done.22), channel_id=1, source_target_pairs={{0,2},{1,3},{2,4},{3,5},{4,6},{5,7},{6,0},{7,1},{8,14},{9,15},{10,... | collective-permute-start | bytes 1572872 | tf_op jit(solution)/shard_map/ppermute | solution.py:58
  70.8 16.5 %collective-permute-start.9 = (bf16[512,1024]{1,0:T(8,128)(2,1)S(1)}, bf16[512,1024]{1,0:T(8,128)(2,1)}, u32[]{:S(2)}, u32[]{:S(2)}) collective-permute-start(bf16[512,1024]{1,0:T(8,128)(2,1)S(1)} %collective-permute-done.5.refs_6_), channel_id=1, source_target_pairs={{0,16},{1,17},{2,18},{3,19},{4,20},{5,21},{6,22},{7,23},{8,56},{9,... | collective-permute-start | bytes 3145736 | tf_op jit(solution)/shard_map/ppermute | solution.py:58
  75.7 22.5 %collective-permute-start.6 = (bf16[512,1024]{1,0:T(8,128)(2,1)S(1)}, bf16[512,1024]{1,0:T(8,128)(2,1)}, u32[]{:S(2)}, u32[]{:S(2)}) collective-permute-start(bf16[512,1024]{1,0:T(8,128)(2,1)S(1)} %collective-permute-done.1.refs_5_), channel_id=1, source_target_pairs={{0,16},{1,17},{2,18},{3,19},{4,20},{5,21},{6,22},{7,23},{8,56},{9,... | collective-permute-start | bytes 3145736 | tf_op jit(solution)/shard_map/ppermute | solution.py:58
  81.3 16.9 %collective-permute-start.2 = (bf16[512,1024]{1,0:T(8,128)(2,1)S(1)}, bf16[512,1024]{1,0:T(8,128)(2,1)}, u32[]{:S(2)}, u32[]{:S(2)}) collective-permute-start(bf16[512,1024]{1,0:T(8,128)(2,1)S(1)} %collective-permute-done.1.refs_5_), channel_id=1, source_target_pairs={{0,2},{1,3},{2,4},{3,5},{4,6},{5,7},{6,0},{7,1},{8,14},{9,15},{10,... | collective-permute-start | bytes 3145736 | tf_op jit(solution)/shard_map/ppermute | solution.py:58
  83.0 25.5 %collective-permute-start.4 = (bf16[512,1024]{1,0:T(8,128)(2,1)S(1)}, bf16[512,1024]{1,0:T(8,128)(2,1)S(1)}, u32[]{:S(2)}, u32[]{:S(2)}) collective-permute-start(bf16[512,1024]{1,0:T(8,128)(2,1)S(1)} %collective-permute-done.refs_1_), channel_id=1, source_target_pairs={{0,2},{1,3},{2,4},{3,5},{4,6},{5,7},{6,0},{7,1},{8,14},{9,15},{10,... | collective-permute-start | bytes 3145736 | tf_op jit(solution)/shard_map/ppermute | solution.py:58
  85.1 25.0 %collective-permute-start.8 = (bf16[512,1024]{1,0:T(8,128)(2,1)S(1)}, bf16[512,1024]{1,0:T(8,128)(2,1)S(1)}, u32[]{:S(2)}, u32[]{:S(2)}) collective-permute-start(bf16[512,1024]{1,0:T(8,128)(2,1)S(1)} %collective-permute-done.5.refs_6_), channel_id=1, source_target_pairs={{0,8},{1,9},{2,10},{3,11},{4,12},{5,13},{6,14},{7,15},{8,0},{9,1},... | collective-permute-start | bytes 3145736 | tf_op jit(solution)/shard_map/ppermute | solution.py:58
  87.4 33.4 %collective-permute-start.14 = (bf16[512,1024]{1,0:T(8,128)(2,1)S(1)}, bf16[512,1024]{1,0:T(8,128)(2,1)}, u32[]{:S(2)}, u32[]{:S(2)}) collective-permute-start(bf16[512,1024]{1,0:T(8,128)(2,1)S(1)} %collective-permute-done.12.refs_13_.refs_8_), channel_id=1, source_target_pairs={{0,16},{1,17},{2,18},{3,19},{4,20},{5,21},{6,22},{7,23},{8,56},{9,... | collective-permute-start | bytes 3145736 | tf_op jit(solution)/shard_map/ppermute | solution.py:58
  98.2 23.1 %collective-permute-start.10 = (bf16[512,1024]{1,0:T(8,128)(2,1)}, bf16[512,1024]{1,0:T(8,128)(2,1)}, u32[]{:S(2)}, u32[]{:S(2)}) collective-permute-start(bf16[512,1024]{1,0:T(8,128)(2,1)} %collective-permute-done.9.refs_10_), channel_id=1, source_target_pairs={{0,8},{1,9},{2,10},{3,11},{4,12},{5,13},{6,14},{7,15},{8,0},{9,1},... | collective-permute-start | bytes 3145736 | tf_op jit(solution)/shard_map/ppermute | solution.py:58
  98.2 23.7 %collective-permute-start.7 = (bf16[512,1024]{1,0:T(8,128)(2,1)}, bf16[512,1024]{1,0:T(8,128)(2,1)}, u32[]{:S(2)}, u32[]{:S(2)}) collective-permute-start(bf16[512,1024]{1,0:T(8,128)(2,1)} %collective-permute-done.6.refs_7_), channel_id=1, source_target_pairs={{0,8},{1,9},{2,10},{3,11},{4,12},{5,13},{6,14},{7,15},{8,0},{9,1},... | collective-permute-start | bytes 3145736 | tf_op jit(solution)/shard_map/ppermute | solution.py:58
  108.5 16.1 %collective-permute-start.28 = (bf16[512,1024]{1,0:T(8,128)(2,1)S(1)}, bf16[512,1024]{1,0:T(8,128)(2,1)}, u32[]{:S(2)}, u32[]{:S(2)}) collective-permute-start(bf16[512,1024]{1,0:T(8,128)(2,1)S(1)} %collective-permute-done.13.refs_14_.refs_9_), channel_id=1, source_target_pairs={{0,16},{1,17},{2,18},{3,19},{4,20},{5,21},{6,22},{7,23},{8,56},{9,... | collective-permute-start | bytes 3145736 | tf_op jit(solution)/shard_map/ppermute | solution.py:58
  120.8 40.8 %collective-permute-start.27 = (bf16[512,1024]{1,0:T(8,128)(2,1)S(1)}, bf16[512,1024]{1,0:T(8,128)(2,1)}, u32[]{:S(2)}, u32[]{:S(2)}) collective-permute-start(bf16[512,1024]{1,0:T(8,128)(2,1)S(1)} %collective-permute-done.13.refs_14_.refs_9_), channel_id=1, source_target_pairs={{0,8},{1,9},{2,10},{3,11},{4,12},{5,13},{6,14},{7,15},{8,0},{9,1},... | collective-permute-start | bytes 3145736 | tf_op jit(solution)/shard_map/ppermute | solution.py:58
  121.3 40.4 %collective-permute-start.25 = (bf16[512,1024]{1,0:T(8,128)(2,1)}, bf16[512,1024]{1,0:T(8,128)(2,1)}, u32[]{:S(2)}, u32[]{:S(2)}) collective-permute-start(bf16[512,1024]{1,0:T(8,128)(2,1)} %copy-done.7), channel_id=1, source_target_pairs={{0,1},{1,0},{2,3},{3,2},{4,5},{5,4},{6,7},{7,6},{8,9},{9,8},{10,11... | collective-permute-start | bytes 3145736 | tf_op jit(solution)/shard_map/ppermute | solution.py:58
  121.9 39.8 %collective-permute-start.26 = (bf16[512,1024]{1,0:T(8,128)(2,1)}, bf16[512,1024]{1,0:T(8,128)(2,1)}, u32[]{:S(2)}, u32[]{:S(2)}) collective-permute-start(bf16[512,1024]{1,0:T(8,128)(2,1)} %collective-permute-done.14.refs_15_.refs_10_), channel_id=1, source_target_pairs={{0,8},{1,9},{2,10},{3,11},{4,12},{5,13},{6,14},{7,15},{8,0},{9,1},... | collective-permute-start | bytes 3145736 | tf_op jit(solution)/shard_map/ppermute | solution.py:58
  124.6 37.0 %collective-permute-start.29 = (bf16[512,1024]{1,0:T(8,128)(2,1)}, bf16[512,1024]{1,0:T(8,128)(2,1)}, u32[]{:S(2)}, u32[]{:S(2)}) collective-permute-start(bf16[512,1024]{1,0:T(8,128)(2,1)} %collective-permute-done.28.refs_13_), channel_id=1, source_target_pairs={{0,8},{1,9},{2,10},{3,11},{4,12},{5,13},{6,14},{7,15},{8,0},{9,1},... | collective-permute-start | bytes 3145736 | tf_op jit(solution)/shard_map/ppermute | solution.py:58
  124.8 36.8 %collective-permute-start.24 = (bf16[256,1024]{1,0:T(8,128)(2,1)}, bf16[256,1024]{1,0:T(8,128)(2,1)}, u32[]{:S(2)}, u32[]{:S(2)}) collective-permute-start(bf16[256,1024]{1,0:T(8,128)(2,1)} %copy-done.22), channel_id=1, source_target_pairs={{0,8},{1,9},{2,10},{3,11},{4,12},{5,13},{6,14},{7,15},{8,0},{9,1},... | collective-permute-start | bytes 1572872 | tf_op jit(solution)/shard_map/ppermute | solution.py:58
  129.0 18.3 %all-to-all-start.1 = ((f32[8,8,128]{2,1,0:T(8,128)}), f32[8,8,128]{2,1,0:T(8,128)S(1)}, u32[]{:S(2)}, u32[]{:S(2)}) async-start(f32[8,8,128]{2,1,0:T(8,128)} %broadcast_in_dim.23), calls=%async_computation.1 | async-start | bytes 65536 | tf_op jit(solution)/shard_map/all_to_all | solution.py:332
  182.0 29.0 %all-to-all-start.2 = ((f16[16,512,128]{2,1,0:T(8,128)(2,1)}), f16[16,512,128]{2,1,0:T(8,128)(2,1)S(1)}, u32[]{:S(2)}, u32[]{:S(2)}) async-start(f16[16,512,128]{2,1,0:T(8,128)(2,1)} %convert_element_type.6), calls=%async_computation.2 | async-start | bytes 4194304 | tf_op jit(solution)/shard_map/all_to_all | solution.py:355
  (36 other events, 293.5 us)
